TPU v7x, 256 devices: a whole 4x4x8 slice. The times are simulated.
256 devices in a mesh: aux: 16 (over x, z_hi), pair: 16 (over y, z_lo, core).
Axes of the slice: x: 4, y: 4, z: 8 (z_hi: 4, z_lo: 2; z = z_hi * 2 + z_lo), core: 2. Of those that a mesh axis runs over, the one named last changes fastest.
Arguments:
- amplitudes: bfloat16 [512, 36864], P(('aux', 'pair')), may hold values from -6 to 6
- factors: bfloat16 [256, 36864], P('aux'), may hold values from -0.109375 to 0.109375
- sources: int32 [512, 8], P(('aux', 'pair')), may hold values from 0 to 511, as said below
- weights: float32 [512, 8], P(('aux', 'pair')), may hold values from -0.5 to 0.5
- flip_flags: int32 [512, 8], P(('aux', 'pair')), may hold values 0 or 1
Outputs:
- residual: float32 [512, 36864], P(('aux', 'pair'))
Inputs may be any that keep to these rules, and one draw needn't show every extreme that they name: `sources`: every source lies in the same aligned block of 32 pairs as its target pair.
All inputs are finite; a program needn't handle non-finite values. No bound on the sum of `flip_flags` on one device may be relied on, other than what follows from the above.
Results may differ from a plain program's by a relative error of at most 0.0026.
Values may be sent and summed in bfloat16 or wider, within the bound.
No kernel may reach another device: no remote copies, remote signals or barrier semaphores. Data moves between devices by JAX's collectives and lax.ppermute only.
A program may use at most 128 MiB of HBM per device.

v0:
```python
import jax
import jax.numpy as jnp
from jax import lax
from jax.experimental import pallas as pl
from jax.experimental.pallas import tpu as pltpu
from jax.sharding import PartitionSpec as P


V = 192
W = 2 * V
TILES = V * V // 128
X, ZH, Y, ZL, C = 4, 4, 4, 2, 2


VMEM = pl.BlockSpec(memory_space=pltpu.VMEM)
SMEM = pl.BlockSpec(memory_space=pltpu.SMEM)


def params(mib):
    return pltpu.CompilerParams(vmem_limit_bytes=mib << 20)


def cost(flops, bytes_accessed):
    return pl.CostEstimate(flops=flops, bytes_accessed=bytes_accessed, transcendentals=0)


def aux_shift(dx, dz):
    return [(x * ZH + z, (x + dx) % X * ZH + (z + dz) % ZH) for x in range(X) for z in range(ZH)]


def pair_flip(mask):
    return [(p, p ^ mask) for p in range(Y * ZL * C)]


def turn(tile):
    return jnp.concatenate([tile[:, 64:], tile[:, :64]], axis=1)


def low_lanes(rows):
    return lax.broadcasted_iota(jnp.int32, (rows, 128), 1) < 64


def write_pack(source, pitch, first, lines, put):
    half = V // 2
    low = low_lanes(half)

    def strip(row, j):
        return source[pl.ds(pitch * j + row, half, stride=3 * pitch), :]

    for side in range(2):
        s1, s2 = turn(strip(first + side, 1)), turn(strip(first + side, 2))
        lines[side, pl.ds(0, half, stride=2), :] = strip(first + side, 0)
        lines[side, pl.ds(1, half, stride=2), :] = jnp.where(low, s1, s2)
    lines[2, pl.ds(0, half, stride=2), :] = jnp.where(low, strip(first, 1), turn(strip(first + 1, 1)))
    lines[2, pl.ds(1, half, stride=2), :] = jnp.where(low, turn(strip(first, 2)), strip(first + 1, 2))
    for t in range(3):
        put(t, lines[t].astype(jnp.bfloat16))


def prep_amp_kernel(amp_ref, pack_ref, flat, lines):
    for k in range(TILES):
        flat[8 * k : 8 * k + 2, :] = amp_ref[:, 128 * k : 128 * k + 128].astype(jnp.float32)

    def put(t, value):
        pack_ref[:, 128 * t : 128 * t + 128] = value

    write_pack(flat, 8, 0, lines, put)


def prep_fac_kernel(core_ref, fac_ref, own_ref, other_ref, flat, lines):
    for k in range(TILES):
        flat[16 * k : 16 * k + 16, :] = fac_ref[:, 128 * k : 128 * k + 128].astype(jnp.float32)
    core = core_ref[0]
    for place, target in ((core, own_ref), (1 - core, other_ref)):
        for q in range(4):

            def put(t, value, target=target, q=q):
                target[q, :, 128 * t : 128 * t + 128] = value

            write_pack(flat, 16, 8 * place + 2 * q, lines.at[q], put)


def prep_amp(amplitudes):
    return pl.pallas_call(
        prep_amp_kernel,
        out_shape=jax.ShapeDtypeStruct((V, W), jnp.bfloat16),
        in_specs=[VMEM],
        out_specs=VMEM,
        scratch_shapes=[
            pltpu.VMEM((8 * TILES, 128), jnp.float32),
            pltpu.VMEM((3, V, 128), jnp.float32),
        ],
        compiler_params=params(12),
        cost_estimate=cost(0, 2 << 20),
        name="prep_amp",
    )(amplitudes)


def prep_fac(core, factors):
    packs = jax.ShapeDtypeStruct((4, V, W), jnp.bfloat16)
    return pl.pallas_call(
        prep_fac_kernel,
        out_shape=(packs, packs),
        in_specs=[SMEM, VMEM],
        out_specs=(VMEM, VMEM),
        scratch_shapes=[
            pltpu.VMEM((16 * TILES, 128), jnp.float32),
            pltpu.VMEM((4, 3, V, 128), jnp.float32),
        ],
        compiler_params=params(16),
        cost_estimate=cost(0, 6 << 20),
        name="prep_fac",
    )(core, factors)


def ladder_step(amps, facs, add, low):
    stacked_even = jnp.concatenate(
        [jnp.concatenate([f[:, 0:128], f[:, 256:320]], axis=1) for f in facs], axis=0
    )
    stacked_odd = jnp.concatenate(
        [jnp.concatenate([f[:, 128:256], f[:, 320:384]], axis=1) for f in facs], axis=0
    )
    wide = jnp.concatenate(amps, axis=1)
    even = jnp.dot(stacked_even, wide, preferred_element_type=jnp.float32).astype(jnp.bfloat16)
    odd = jnp.dot(stacked_odd, wide, preferred_element_type=jnp.float32).astype(jnp.bfloat16)
    rows = []
    for p in range(len(amps)):
        first, second = [], []
        for q in range(len(facs)):
            e = even[q * V : (q + 1) * V, p * W : (p + 1) * W]
            o = odd[q * V : (q + 1) * V, p * W : (p + 1) * W]
            first += [e[:, 0:128], o[:, 0:128], jnp.where(low, e[:, 256:], turn(o[:, 256:]))]
            second += [e[:, 128:256], o[:, 128:256], jnp.where(low, turn(e[:, 256:]), o[:, 256:])]
        rows += [jnp.concatenate(first, axis=1), jnp.concatenate(second, axis=1)]
    halfway = jnp.concatenate(rows, axis=0)
    turned = jnp.concatenate(facs, axis=1)
    out = lax.dot_general(
        halfway, turned, (((1,), (1,)), ((), ())), preferred_element_type=jnp.float32
    )
    for p in range(len(amps)):
        a, b = out[2 * p * V : (2 * p + 1) * V], out[(2 * p + 1) * V : (2 * p + 2) * V]
        add(p, 0, a[:, 0:128])
        add(p, 1, b[:, 0:128])
        add(p, 2, jnp.concatenate([a[:, 128:V], b[:, 128:V]], axis=1))


def ladder(amps, facs, carried, narrow, deep):
    count, arrays = len(amps), sum(f.shape[0] // 4 for f in facs)
    held = []
    for array, _ in carried:
        if not any(array is h for h in held):
            held.append(array)
    places = [([array is h for h in held].index(True), at) for array, at in carried]
    ins = count + len(facs) + len(held)

    def kernel(*refs):
        amp_refs, fac_refs = refs[:count], refs[count : count + len(facs)]
        held_refs, outs = refs[count + len(facs) : ins], refs[ins:]
        total = outs[-1]
        low = low_lanes(V)
        for p in range(count):
            if places:
                total[p] = held_refs[places[p][0]][places[p][1]]
            else:
                total[p] = jnp.zeros((V, W), jnp.float32)

        def add(p, t, value):
            total[p, :, 128 * t : 128 * t + 128] += value

        for fac in fac_refs:

            def step(s, none, fac=fac):
                ladder_step([a[...] for a in amp_refs], [fac[s * deep + i] for i in range(deep)], add, low)
                return none

            lax.fori_loop(0, fac.shape[0] // deep, step, 0)
        if narrow:
            for p in range(count):
                outs[p][...] = total[p].astype(jnp.bfloat16)

    if narrow:
        shapes = tuple(jax.ShapeDtypeStruct((V, W), jnp.bfloat16) for _ in range(count))
        specs, scratch = (VMEM,) * count, [pltpu.VMEM((count, V, W), jnp.float32)]
    else:
        shapes, specs, scratch = jax.ShapeDtypeStruct((count, V, W), jnp.float32), VMEM, []
    return pl.pallas_call(
        kernel,
        out_shape=shapes,
        in_specs=[VMEM] * ins,
        out_specs=specs,
        scratch_shapes=scratch,
        compiler_params=params(24),
        cost_estimate=cost(count * arrays * 16 * 4 * V**3 * 2, 1 << 20),
    )(*amps, *facs, *held)


def couple_kernel(where_ref, sources_ref, weights_ref, flips_ref, near_ref, far_ref, out_ref, sums):
    sums[...] = jnp.zeros_like(sums)
    lane = lax.broadcasted_iota(jnp.int32, (V, 128), 1)

    def slot(s, none):
        p, k = s // 8, s % 8
        local = lax.rem(sources_ref[p, k], 2 * Y * ZL * C)
        side = lax.rem(local, 2)
        apart = (local // 2) ^ where_ref[0]
        core, rest = lax.rem(apart, 2), apart // 2
        flip = flips_ref[p, k]
        weight = weights_ref[p, k]
        mixed = jnp.where((lane // 64) == side, weight, 0.0)

        def gather(ref):
            main = ref[rest, :, pl.ds(pl.multiple_of(side * 128, 128), 128)].astype(jnp.float32)
            shared = ref[rest, :, 256:384].astype(jnp.float32)
            sums[p, flip, 0, 0:V, :] += weight * main
            sums[p, flip, 1, 0:V, :] += mixed * shared

        @pl.when(core == 0)
        def _():
            gather(near_ref)

        @pl.when(core == 1)
        def _():
            gather(far_ref)

        return none

    lax.fori_loop(0, 16, slot, 0)
    shared = []
    for p in range(2):
        plain, tail = sums[p, 0, 0, 0:V, :], sums[p, 0, 1, 0:V, :]
        tail = tail + turn(tail)
        turned_tail = sums[p, 1, 1]
        top = sums[p, 1, 0].T
        bottom = (turned_tail + turn(turned_tail)).T
        out_ref[0:128, 128 * p : 128 * p + 128] = plain[0:128] + top[:, 0:128]
        out_ref[128:V, 128 * p : 128 * p + 128] = plain[128:V] + bottom[0:64, 0:128]
        right = jnp.concatenate([top[:, 128:256], bottom[0:64, 128:256]], axis=0)
        shared.append(tail + (right if p == 0 else turn(right)))
    out_ref[:, 256:384] = jnp.where(lane < 64, shared[0], shared[1])


def couple(where, sources, weights, flips, near, far):
    return pl.pallas_call(
        couple_kernel,
        out_shape=jax.ShapeDtypeStruct((V, W), jnp.float32),
        in_specs=[SMEM] * 4 + [VMEM] * 2,
        out_specs=VMEM,
        scratch_shapes=[pltpu.VMEM((2, 2, 2, 256, 128), jnp.float32)],
        compiler_params=params(12),
        cost_estimate=cost(1 << 20, 4 << 20),
        name="couple",
    )(where, sources, weights, flips, near, far)


def finish_kernel(own_ref, couple_ref, a_ref, b_ref, c_ref, out_ref, total, flat):
    half = V // 2
    low = low_lanes(half)
    for t in range(3):
        cut = slice(128 * t, 128 * t + 128)
        total[t] = (own_ref[0, :, cut] + couple_ref[:, cut]) + (
            (a_ref[:, cut].astype(jnp.float32) + b_ref[:, cut].astype(jnp.float32))
            + c_ref[:, cut].astype(jnp.float32)
        )

    def line(t, odd):
        return total[t, pl.ds(odd, half, stride=2), :]

    for p in range(2):
        even, odd = line(2, 0), line(2, 1)
        main = turn(line(p, 1))
        flat[pl.ds(p, half, stride=24), :] = line(p, 0)
        flat[pl.ds(8 + p, half, stride=24), :] = jnp.where(low, even if p == 0 else turn(even), main)
        flat[pl.ds(16 + p, half, stride=24), :] = jnp.where(low, main, turn(odd) if p == 0 else odd)
    for k in range(TILES):
        out_ref[:, 128 * k : 128 * k + 128] = flat[8 * k : 8 * k + 2, :]


def finish(own, coupled, parts):
    return pl.pallas_call(
        finish_kernel,
        out_shape=jax.ShapeDtypeStruct((2, V * V), jnp.float32),
        in_specs=[VMEM] * 5,
        out_specs=VMEM,
        scratch_shapes=[
            pltpu.VMEM((3, V, 128), jnp.float32),
            pltpu.VMEM((8 * TILES, 128), jnp.float32),
        ],
        compiler_params=params(12),
        cost_estimate=cost(1 << 20, 2 << 20),
        name="finish",
    )(own, coupled, *parts)


def local(amplitudes, factors, sources, weights, flips):
    where = lax.axis_index("pair").astype(jnp.int32).reshape(1)

    def aux(value, dx, dz):
        return lax.ppermute(value, "aux", aux_shift(dx, dz))

    def pair(value, mask):
        return lax.ppermute(value, "pair", pair_flip(mask))

    pack = prep_amp(amplitudes)
    across, below, above = aux(pack, 0, 2), aux(pack, 0, 1), aux(pack, 0, 3)
    own, other = prep_fac(where % C, factors)
    left, right = aux(own, 1, 0), aux(own, 3, 0)
    self_total = ladder([pack], [own, other], [], False, 4)
    facing = aux(own, 2, 0)
    mates = jnp.stack([pack, pair(pack, 2)])
    rest = [across, below, above]
    total = ladder(rest, [own, other], [], False, 4)
    mates = jnp.concatenate([mates, pair(mates, 4)])
    sides_other = pair(jnp.concatenate([left, right]), 1)
    carried = [(total, 0), (total, 1), (total, 2), (self_total, 0)]
    total4 = ladder(rest + [pack], [left, right], carried, False, 2)
    near = jnp.concatenate([mates, pair(mates, 8)])
    total = ladder(rest, [sides_other], [(total4, i) for i in range(3)], False, 4)
    facing_other = pair(facing, 1)
    total = ladder(rest, [facing], [(total, i) for i in range(3)], False, 4)
    far = pair(near, 1)
    back = ladder(rest, [facing_other], [(total, i) for i in range(3)], True, 4)
    parts = (aux(back[0], 0, 2), aux(back[1], 0, 3), aux(back[2], 0, 1))
    mine = ladder([pack], [sides_other, facing, facing_other], [(total4, 3)], False, 4)
    coupled = couple(where, sources, weights, flips, near, far)
    return finish(mine, coupled, parts)


def solution(mesh):
    placed = (
        P(("aux", "pair"), None),
        P("aux", None),
        P(("aux", "pair"), None),
        P(("aux", "pair"), None),
        P(("aux", "pair"), None),
    )
    return jax.shard_map(
        local, mesh=mesh, in_specs=placed, out_specs=P(("aux", "pair"), None), check_vma=False
    )
```

profile of v0, /device:TPU:1, one launch (start us, length us, event | category | flops | bytes accessed | tf_op | source)
XLA Modules:
  0.0 91.6 jit_solution(8964480228978018268)
XLA Ops:
  0.0 1.3 %copy-done = bf16[16,36864]{1,0:T(8,128)(2,1)S(1)} copy-done((bf16[16,36864]{1,0:T(8,128)(2,1)S(1)}, bf16[16,36864]{1,0:T(8,128)(2,1)}, u32[]{:S(2)}) %copy-start) | copy-done | bytes 1179672
  1.3 1.8 %prep_fac.1 = (bf16[4,192,384]{2,1,0:T(8,128)(2,1)S(1)}, bf16[4,192,384]{2,1,0:T(8,128)(2,1)S(1)}) custom-call(s32[1]{0:T(128)S(6)} %select_n.7.core_ref, bf16[16,36864]{1,0:T(8,128)(2,1)S(1)} %copy-done), custom_call_target="tpu_custom_call" | custom-call | bytes 6291456 | tf_op jit(solution)/shard_map/prep_fac/pallas_call | solution.py:101
  3.1 3.4 %collective-permute-start.1 = (bf16[4,192,384]{2,1,0:T(8,128)(2,1)S(1)}, bf16[4,192,384]{2,1,0:T(8,128)(2,1)S(1)}, u32[]{:S(2)}, u32[]{:S(2)}) collective-permute-start(bf16[4,192,384]{2,1,0:T(8,128)(2,1)S(1)} %get-tuple-element.10.refs_3_.refs_1_), channel_id=1, source_target_pairs={{0,192},{16,208},{32,224},{48,240},{64,0},{80,16},{96,32},{112,48}... | collective-permute-start | bytes 1769480 | tf_op jit(solution)/shard_map/ppermute | solution.py:298
  6.5 0.2 prep_amp.1.refs_0_.refs_3_
  6.7 1.7 %collective-permute-start.8 = (bf16[192,384]{1,0:T(8,128)(2,1)S(1)}, bf16[192,384]{1,0:T(8,128)(2,1)S(1)}, u32[]{:S(2)}, u32[]{:S(2)}) collective-permute-start(bf16[192,384]{1,0:T(8,128)(2,1)S(1)} %prep_amp.1.refs_0_.refs_3_), channel_id=1, source_target_pairs={{0,2},{1,3},{2,0},{3,1},{4,6},{5,7},{6,4},{7,5},{8,10},{9,11},{10,... | collective-permute-start | bytes 442376 | tf_op jit(solution)/shard_map/ppermute | solution.py:301
  8.4 5.1 %collective-permute-start.7 = (bf16[192,384]{1,0:T(8,128)(2,1)S(1)}, bf16[192,384]{1,0:T(8,128)(2,1)S(1)}, u32[]{:S(2)}, u32[]{:S(2)}) collective-permute-start(bf16[192,384]{1,0:T(8,128)(2,1)S(1)} %prep_amp.1.refs_0_.refs_3_), channel_id=1, source_target_pairs={{0,48},{16,0},{32,16},{48,32},{64,112},{80,64},{96,80},{112,96},{1... | collective-permute-start | bytes 442376 | tf_op jit(solution)/shard_map/ppermute | solution.py:298
  13.5 0.0 collective-permute-start.6
  13.5 2.1 %shard_map.56.refs_7_ = f32[1,192,384]{2,1,0:T(8,128)S(1)} custom-call(bf16[192,384]{1,0:T(8,128)(2,1)S(1)} %prep_amp.1.refs_0_.refs_3_, bf16[4,192,384]{2,1,0:T(8,128)(2,1)S(1)} %get-tuple-element.10.refs_3_.refs_1_, bf16[4,192,384]{2,1,0:T(8,128)(2,1)S(1)} %get-tuple-element.11.refs_4_.refs_2_), custom_call_target="tpu_custom_call" | custom-call | flops 1811939328 | bytes 1048576 | tf_op jit(solution)/shard_map/pallas_call | solution.py:186
  15.7 0.0 collective-permute-done.8
  15.7 3.3 %collective-permute-start.5 = (bf16[192,384]{1,0:T(8,128)(2,1)S(1)}, bf16[192,384]{1,0:T(8,128)(2,1)S(1)}, u32[]{:S(2)}, u32[]{:S(2)}) collective-permute-start(bf16[192,384]{1,0:T(8,128)(2,1)S(1)} %prep_amp.1.refs_0_.refs_3_), channel_id=1, source_target_pairs={{0,32},{16,48},{32,0},{48,16},{64,96},{80,112},{96,64},{112,80},{1... | collective-permute-start | bytes 442376 | tf_op jit(solution)/shard_map/ppermute | solution.py:298
  19.1 1.8 %collective-permute-start.3 = (bf16[4,192,384]{2,1,0:T(8,128)(2,1)S(1)}, bf16[4,192,384]{2,1,0:T(8,128)(2,1)S(1)}, u32[]{:S(2)}, u32[]{:S(2)}) collective-permute-start(bf16[4,192,384]{2,1,0:T(8,128)(2,1)S(1)} %get-tuple-element.10.refs_3_.refs_1_), channel_id=1, source_target_pairs={{0,128},{16,144},{32,160},{48,176},{64,192},{80,208},{96,224},{112... | collective-permute-start | bytes 1769480 | tf_op jit(solution)/shard_map/ppermute | solution.py:298
  20.9 0.7 collective-permute-done.refs_4_
  21.6 1.3 %collective-permute-start.9 = (bf16[2,192,384]{2,1,0:T(8,128)(2,1)S(1)}, bf16[2,192,384]{2,1,0:T(8,128)(2,1)S(1)}, u32[]{:S(2)}, u32[]{:S(2)}) collective-permute-start(bf16[2,192,384]{2,1,0:T(8,128)(2,1)S(1)} %pad_maximum_fusion.3), channel_id=1, source_target_pairs={{0,4},{1,5},{2,6},{3,7},{4,0},{5,1},{6,2},{7,3},{8,12},{9,13},{10,... | collective-permute-start | bytes 884744 | tf_op jit(solution)/shard_map/ppermute | solution.py:301
  22.9 0.1 pad_maximum_fusion
  23.0 6.7 %collective-permute-start.2 = (bf16[8,192,384]{2,1,0:T(8,128)(2,1)S(1)}, bf16[8,192,384]{2,1,0:T(8,128)(2,1)S(1)}, u32[]{:S(2)}, u32[]{:S(2)}) collective-permute-start(bf16[8,192,384]{2,1,0:T(8,128)(2,1)S(1)} %pad_maximum_fusion), channel_id=1, source_target_pairs={{0,1},{1,0},{2,3},{3,2},{4,5},{5,4},{6,7},{7,6},{8,9},{9,8},{10,11... | collective-permute-start | bytes 3538952 | tf_op jit(solution)/shard_map/ppermute | solution.py:301
  29.7 4.6 %shard_map.55.refs_6_ = f32[3,192,384]{2,1,0:T(8,128)S(1)} custom-call(bf16[192,384]{1,0:T(8,128)(2,1)S(1)} %collective-permute-done.5.refs_0_, bf16[192,384]{1,0:T(8,128)(2,1)S(1)} %collective-permute-done.6.refs_1_, bf16[192,384]{1,0:T(8,128)(2,1)S(1)} %collective-permute-done.7.refs_2_, bf16[4,192,384]{2,1,0:T(8,128)(2,1)S(1)} %get-tuple-element.10.refs_3_.refs_1_, ...), custom_call_target="tpu_custom_call" | custom-call | flops 5435817984 | bytes 1048576 | tf_op jit(solution)/shard_map/pallas_call | solution.py:186
  34.3 0.1 pad_maximum_fusion.2
  34.4 2.7 %collective-permute-start.10 = (bf16[4,192,384]{2,1,0:T(8,128)(2,1)S(1)}, bf16[4,192,384]{2,1,0:T(8,128)(2,1)S(1)}, u32[]{:S(2)}, u32[]{:S(2)}) collective-permute-start(bf16[4,192,384]{2,1,0:T(8,128)(2,1)S(1)} %pad_maximum_fusion.2), channel_id=1, source_target_pairs={{0,8},{1,9},{2,10},{3,11},{4,12},{5,13},{6,14},{7,15},{8,0},{9,1},... | collective-permute-start | bytes 1769480 | tf_op jit(solution)/shard_map/ppermute | solution.py:301
  37.1 2.8 %collective-permute-start.4 = (bf16[4,192,384]{2,1,0:T(8,128)(2,1)S(1)}, bf16[4,192,384]{2,1,0:T(8,128)(2,1)S(1)}, u32[]{:S(2)}, u32[]{:S(2)}) collective-permute-start(bf16[4,192,384]{2,1,0:T(8,128)(2,1)S(1)} %collective-permute-done.3.refs_2_.refs_3_), channel_id=1, source_target_pairs={{0,1},{1,0},{2,3},{3,2},{4,5},{5,4},{6,7},{7,6},{8,9},{9,8},{10,11... | collective-permute-start | bytes 1769480 | tf_op jit(solution)/shard_map/ppermute | solution.py:301
  39.9 5.9 %shard_map.57.refs_4_ = f32[4,192,384]{2,1,0:T(8,128)S(1)} custom-call(bf16[192,384]{1,0:T(8,128)(2,1)S(1)} %collective-permute-done.5.refs_0_, bf16[192,384]{1,0:T(8,128)(2,1)S(1)} %collective-permute-done.6.refs_1_, bf16[192,384]{1,0:T(8,128)(2,1)S(1)} %collective-permute-done.7.refs_2_, bf16[192,384]{1,0:T(8,128)(2,1)S(1)} %prep_amp.1.refs_0_.refs_3_, ...), custom_call_target="tpu_custom_call" | custom-call | flops 7247757312 | bytes 1048576 | tf_op jit(solution)/shard_map/pallas_call | solution.py:186
  45.8 2.8 %collective-permute-done.10 = bf16[4,192,384]{2,1,0:T(8,128)(2,1)S(1)} collective-permute-done((bf16[4,192,384]{2,1,0:T(8,128)(2,1)S(1)}, bf16[4,192,384]{2,1,0:T(8,128)(2,1)S(1)}, u32[]{:S(2)}, u32[]{:S(2)}) %collective-permute-start.10) | collective-permute-done | bytes 589856 | tf_op jit(solution)/shard_map/ppermute | solution.py:301
  48.6 0.2 pad_maximum_fusion.1.near_ref
  48.8 3.4 %collective-permute-start.11 = (bf16[8,192,384]{2,1,0:T(8,128)(2,1)S(1)}, bf16[8,192,384]{2,1,0:T(8,128)(2,1)S(1)}, u32[]{:S(2)}, u32[]{:S(2)}) collective-permute-start(bf16[8,192,384]{2,1,0:T(8,128)(2,1)S(1)} %pad_maximum_fusion.1.near_ref), channel_id=1, source_target_pairs={{0,1},{1,0},{2,3},{3,2},{4,5},{5,4},{6,7},{7,6},{8,9},{9,8},{10,11... | collective-permute-start | bytes 3538952 | tf_op jit(solution)/shard_map/ppermute | solution.py:301
  52.2 4.4 %shard_map.59.refs_4_ = f32[3,192,384]{2,1,0:T(8,128)S(1)} custom-call(bf16[192,384]{1,0:T(8,128)(2,1)S(1)} %collective-permute-done.5.refs_0_, bf16[192,384]{1,0:T(8,128)(2,1)S(1)} %collective-permute-done.6.refs_1_, bf16[192,384]{1,0:T(8,128)(2,1)S(1)} %collective-permute-done.7.refs_2_, bf16[8,192,384]{2,1,0:T(8,128)(2,1)S(1)} %collective-permute-done.2.refs_1_.refs_3_, ...), custom_call_target="tpu_custom_call" | custom-call | flops 5435817984 | bytes 1048576 | tf_op jit(solution)/shard_map/pallas_call | solution.py:186
  56.6 2.2 %shard_map.60.refs_4_ = f32[3,192,384]{2,1,0:T(8,128)S(1)} custom-call(bf16[192,384]{1,0:T(8,128)(2,1)S(1)} %collective-permute-done.5.refs_0_, bf16[192,384]{1,0:T(8,128)(2,1)S(1)} %collective-permute-done.6.refs_1_, bf16[192,384]{1,0:T(8,128)(2,1)S(1)} %collective-permute-done.7.refs_2_, bf16[4,192,384]{2,1,0:T(8,128)(2,1)S(1)} %collective-permute-done.3.refs_2_.refs_3_, ...), custom_call_target="tpu_custom_call" | custom-call | flops 2717908992 | bytes 1048576 | tf_op jit(solution)/shard_map/pallas_call | solution.py:186
  58.8 2.2 %shard_map.61 = (bf16[192,384]{1,0:T(8,128)(2,1)S(1)}, bf16[192,384]{1,0:T(8,128)(2,1)S(1)}, bf16[192,384]{1,0:T(8,128)(2,1)S(1)}) custom-call(bf16[192,384]{1,0:T(8,128)(2,1)S(1)} %collective-permute-done.5.refs_0_, bf16[192,384]{1,0:T(8,128)(2,1)S(1)} %collective-permute-done.6.refs_1_, bf16[192,384]{1,0:T(8,128)(2,1)S(1)} %collective-permute-done.7.refs_2_, ...), custom_call_target="tpu_custom_call" | custom-call | flops 2717908992 | bytes 1048576 | tf_op jit(solution)/shard_map/pallas_call | solution.py:186
  61.0 15.3 %collective-permute-start.12 = (bf16[192,384]{1,0:T(8,128)(2,1)S(1)}, bf16[192,384]{1,0:T(8,128)(2,1)S(1)}, u32[]{:S(2)}, u32[]{:S(2)}) collective-permute-start(bf16[192,384]{1,0:T(8,128)(2,1)S(1)} %get-tuple-element.12), channel_id=1, source_target_pairs={{0,32},{16,48},{32,0},{48,16},{64,96},{80,112},{96,64},{112,80},{1... | collective-permute-start | bytes 442376 | tf_op jit(solution)/shard_map/ppermute | solution.py:298
  76.4 2.4 %collective-permute-start.14 = (bf16[192,384]{1,0:T(8,128)(2,1)S(1)}, bf16[192,384]{1,0:T(8,128)(2,1)S(1)}, u32[]{:S(2)}, u32[]{:S(2)}) collective-permute-start(bf16[192,384]{1,0:T(8,128)(2,1)S(1)} %get-tuple-element.14), channel_id=1, source_target_pairs={{0,16},{16,32},{32,48},{48,0},{64,80},{80,96},{96,112},{112,64},{1... | collective-permute-start | bytes 442376 | tf_op jit(solution)/shard_map/ppermute | solution.py:298
  78.7 5.0 %shard_map.58.own_ref = f32[1,192,384]{2,1,0:T(8,128)S(1)} custom-call(bf16[192,384]{1,0:T(8,128)(2,1)S(1)} %prep_amp.1.refs_0_.refs_3_, bf16[8,192,384]{2,1,0:T(8,128)(2,1)S(1)} %collective-permute-done.2.refs_1_.refs_3_, bf16[4,192,384]{2,1,0:T(8,128)(2,1)S(1)} %collective-permute-done.3.refs_2_.refs_3_, ...), custom_call_target="tpu_custom_call" | custom-call | flops 3623878656 | bytes 1048576 | tf_op jit(solution)/shard_map/pallas_call | solution.py:186
  83.8 2.0 %couple.1.couple_ref = f32[192,384]{1,0:T(8,128)S(1)} custom-call(s32[1]{0:T(128)} %bitcast.where_ref, s32[2,8]{1,0:T(2,128)S(1)} %copy-done.2, f32[2,8]{1,0:T(2,128)S(1)} %copy-done.3, s32[2,8]{1,0:T(2,128)S(1)} %copy-done.4, bf16[8,192,384]{2,1,0:T(8,128)(2,1)S(1)} %pad_maximum_fusion.1.near_ref, bf16[8,192,384]{2,1,0:T(8,128)(2,1)S(1)} %collective-permute-done.11.far_ref), custom_call_target="tpu_custom_call" | custom-call | flops 1048576 | bytes 4194304 | tf_op jit(solution)/shard_map/couple/pallas_call | solution.py:243
  85.8 4.8 %collective-permute-done.13.b_ref = bf16[192,384]{1,0:T(8,128)(2,1)S(1)} collective-permute-done((bf16[192,384]{1,0:T(8,128)(2,1)S(1)}, bf16[192,384]{1,0:T(8,128)(2,1)S(1)}, u32[]{:S(2)}, u32[]{:S(2)}) %collective-permute-start.13) | collective-permute-done | bytes 147488 | tf_op jit(solution)/shard_map/ppermute | solution.py:298
  90.6 1.0 %finish.1 = f32[2,36864]{1,0:T(2,128)} custom-call(f32[1,192,384]{2,1,0:T(8,128)S(1)} %shard_map.58.own_ref, f32[192,384]{1,0:T(8,128)S(1)} %couple.1.couple_ref, bf16[192,384]{1,0:T(8,128)(2,1)S(1)} %collective-permute-done.12.a_ref, bf16[192,384]{1,0:T(8,128)(2,1)S(1)} %collective-permute-done.13.b_ref, bf16[192,384]{1,0:T(8,128)(2,1)S(1)} %collective-permute-done.14.c_ref), custom_call_target="tpu_custom_call" | custom-call | flops 1048576 | bytes 2097152 | tf_op jit(solution)/shard_map/finish/pallas_call | solution.py:279
  (23 shorter events, 0.1 us)
Async XLA Ops:
  0.0 1.3 %copy-start = (bf16[16,36864]{1,0:T(8,128)(2,1)S(1)}, bf16[16,36864]{1,0:T(8,128)(2,1)}, u32[]{:S(2)}) copy-start(bf16[16,36864]{1,0:T(8,128)(2,1)} %fac_ref.1) | copy-start | bytes 3538948
  1.3 5.2 %copy-start.1 = (bf16[2,36864]{1,0:T(2,128)(2,1)S(1)}, bf16[2,36864]{1,0:T(2,128)(2,1)}, u32[]{:S(2)}) copy-start(bf16[2,36864]{1,0:T(2,128)(2,1)} %amp_ref.1) | copy-start | bytes 442372
  3.1 16.0 %collective-permute-start.1 = (bf16[4,192,384]{2,1,0:T(8,128)(2,1)S(1)}, bf16[4,192,384]{2,1,0:T(8,128)(2,1)S(1)}, u32[]{:S(2)}, u32[]{:S(2)}) collective-permute-start(bf16[4,192,384]{2,1,0:T(8,128)(2,1)S(1)} %get-tuple-element.10.refs_3_.refs_1_), channel_id=1, source_target_pairs={{0,192},{16,208},{32,224},{48,240},{64,0},{80,16},{96,32},{112,48}... | collective-permute-start | bytes 1769480 | tf_op jit(solution)/shard_map/ppermute | solution.py:298
  6.5 15.1 %collective-permute-start = (bf16[4,192,384]{2,1,0:T(8,128)(2,1)S(1)}, bf16[4,192,384]{2,1,0:T(8,128)(2,1)S(1)}, u32[]{:S(2)}, u32[]{:S(2)}) collective-permute-start(bf16[4,192,384]{2,1,0:T(8,128)(2,1)S(1)} %get-tuple-element.10.refs_3_.refs_1_), channel_id=1, source_target_pairs={{0,64},{16,80},{32,96},{48,112},{64,128},{80,144},{96,160},{112,17... | collective-permute-start | bytes 1769480 | tf_op jit(solution)/shard_map/ppermute | solution.py:298
  6.7 9.0 %collective-permute-start.8 = (bf16[192,384]{1,0:T(8,128)(2,1)S(1)}, bf16[192,384]{1,0:T(8,128)(2,1)S(1)}, u32[]{:S(2)}, u32[]{:S(2)}) collective-permute-start(bf16[192,384]{1,0:T(8,128)(2,1)S(1)} %prep_amp.1.refs_0_.refs_3_), channel_id=1, source_target_pairs={{0,2},{1,3},{2,0},{3,1},{4,6},{5,7},{6,4},{7,5},{8,10},{9,11},{10,... | collective-permute-start | bytes 442376 | tf_op jit(solution)/shard_map/ppermute | solution.py:301
  8.4 14.6 %collective-permute-start.7 = (bf16[192,384]{1,0:T(8,128)(2,1)S(1)}, bf16[192,384]{1,0:T(8,128)(2,1)S(1)}, u32[]{:S(2)}, u32[]{:S(2)}) collective-permute-start(bf16[192,384]{1,0:T(8,128)(2,1)S(1)} %prep_amp.1.refs_0_.refs_3_), channel_id=1, source_target_pairs={{0,48},{16,0},{32,16},{48,32},{64,112},{80,64},{96,80},{112,96},{1... | collective-permute-start | bytes 442376 | tf_op jit(solution)/shard_map/ppermute | solution.py:298
  13.5 16.2 %collective-permute-start.6 = (bf16[192,384]{1,0:T(8,128)(2,1)S(1)}, bf16[192,384]{1,0:T(8,128)(2,1)S(1)}, u32[]{:S(2)}, u32[]{:S(2)}) collective-permute-start(bf16[192,384]{1,0:T(8,128)(2,1)S(1)} %prep_amp.1.refs_0_.refs_3_), channel_id=1, source_target_pairs={{0,16},{16,32},{32,48},{48,0},{64,80},{80,96},{96,112},{112,64},{1... | collective-permute-start | bytes 442376 | tf_op jit(solution)/shard_map/ppermute | solution.py:298
  15.7 14.0 %collective-permute-start.5 = (bf16[192,384]{1,0:T(8,128)(2,1)S(1)}, bf16[192,384]{1,0:T(8,128)(2,1)S(1)}, u32[]{:S(2)}, u32[]{:S(2)}) collective-permute-start(bf16[192,384]{1,0:T(8,128)(2,1)S(1)} %prep_amp.1.refs_0_.refs_3_), channel_id=1, source_target_pairs={{0,32},{16,48},{32,0},{48,16},{64,96},{80,112},{96,64},{112,80},{1... | collective-permute-start | bytes 442376 | tf_op jit(solution)/shard_map/ppermute | solution.py:298
  19.1 18.0 %collective-permute-start.3 = (bf16[4,192,384]{2,1,0:T(8,128)(2,1)S(1)}, bf16[4,192,384]{2,1,0:T(8,128)(2,1)S(1)}, u32[]{:S(2)}, u32[]{:S(2)}) collective-permute-start(bf16[4,192,384]{2,1,0:T(8,128)(2,1)S(1)} %get-tuple-element.10.refs_3_.refs_1_), channel_id=1, source_target_pairs={{0,128},{16,144},{32,160},{48,176},{64,192},{80,208},{96,224},{112... | collective-permute-start | bytes 1769480 | tf_op jit(solution)/shard_map/ppermute | solution.py:298
  21.6 12.7 %collective-permute-start.9 = (bf16[2,192,384]{2,1,0:T(8,128)(2,1)S(1)}, bf16[2,192,384]{2,1,0:T(8,128)(2,1)S(1)}, u32[]{:S(2)}, u32[]{:S(2)}) collective-permute-start(bf16[2,192,384]{2,1,0:T(8,128)(2,1)S(1)} %pad_maximum_fusion.3), channel_id=1, source_target_pairs={{0,4},{1,5},{2,6},{3,7},{4,0},{5,1},{6,2},{7,3},{8,12},{9,13},{10,... | collective-permute-start | bytes 884744 | tf_op jit(solution)/shard_map/ppermute | solution.py:301
  23.0 29.2 %collective-permute-start.2 = (bf16[8,192,384]{2,1,0:T(8,128)(2,1)S(1)}, bf16[8,192,384]{2,1,0:T(8,128)(2,1)S(1)}, u32[]{:S(2)}, u32[]{:S(2)}) collective-permute-start(bf16[8,192,384]{2,1,0:T(8,128)(2,1)S(1)} %pad_maximum_fusion), channel_id=1, source_target_pairs={{0,1},{1,0},{2,3},{3,2},{4,5},{5,4},{6,7},{7,6},{8,9},{9,8},{10,11... | collective-permute-start | bytes 3538952 | tf_op jit(solution)/shard_map/ppermute | solution.py:301
  34.4 14.3 %collective-permute-start.10 = (bf16[4,192,384]{2,1,0:T(8,128)(2,1)S(1)}, bf16[4,192,384]{2,1,0:T(8,128)(2,1)S(1)}, u32[]{:S(2)}, u32[]{:S(2)}) collective-permute-start(bf16[4,192,384]{2,1,0:T(8,128)(2,1)S(1)} %pad_maximum_fusion.2), channel_id=1, source_target_pairs={{0,8},{1,9},{2,10},{3,11},{4,12},{5,13},{6,14},{7,15},{8,0},{9,1},... | collective-permute-start | bytes 1769480 | tf_op jit(solution)/shard_map/ppermute | solution.py:301
  37.1 21.7 %collective-permute-start.4 = (bf16[4,192,384]{2,1,0:T(8,128)(2,1)S(1)}, bf16[4,192,384]{2,1,0:T(8,128)(2,1)S(1)}, u32[]{:S(2)}, u32[]{:S(2)}) collective-permute-start(bf16[4,192,384]{2,1,0:T(8,128)(2,1)S(1)} %collective-permute-done.3.refs_2_.refs_3_), channel_id=1, source_target_pairs={{0,1},{1,0},{2,3},{3,2},{4,5},{5,4},{6,7},{7,6},{8,9},{9,8},{10,11... | collective-permute-start | bytes 1769480 | tf_op jit(solution)/shard_map/ppermute | solution.py:301
  48.8 34.9 %collective-permute-start.11 = (bf16[8,192,384]{2,1,0:T(8,128)(2,1)S(1)}, bf16[8,192,384]{2,1,0:T(8,128)(2,1)S(1)}, u32[]{:S(2)}, u32[]{:S(2)}) collective-permute-start(bf16[8,192,384]{2,1,0:T(8,128)(2,1)S(1)} %pad_maximum_fusion.1.near_ref), channel_id=1, source_target_pairs={{0,1},{1,0},{2,3},{3,2},{4,5},{5,4},{6,7},{7,6},{8,9},{9,8},{10,11... | collective-permute-start | bytes 3538952 | tf_op jit(solution)/shard_map/ppermute | solution.py:301
  61.0 24.8 %collective-permute-start.12 = (bf16[192,384]{1,0:T(8,128)(2,1)S(1)}, bf16[192,384]{1,0:T(8,128)(2,1)S(1)}, u32[]{:S(2)}, u32[]{:S(2)}) collective-permute-start(bf16[192,384]{1,0:T(8,128)(2,1)S(1)} %get-tuple-element.12), channel_id=1, source_target_pairs={{0,32},{16,48},{32,0},{48,16},{64,96},{80,112},{96,64},{112,80},{1... | collective-permute-start | bytes 442376 | tf_op jit(solution)/shard_map/ppermute | solution.py:298
  76.4 14.3 %collective-permute-start.13 = (bf16[192,384]{1,0:T(8,128)(2,1)S(1)}, bf16[192,384]{1,0:T(8,128)(2,1)S(1)}, u32[]{:S(2)}, u32[]{:S(2)}) collective-permute-start(bf16[192,384]{1,0:T(8,128)(2,1)S(1)} %get-tuple-element.13), channel_id=1, source_target_pairs={{0,48},{16,0},{32,16},{48,32},{64,112},{80,64},{96,80},{112,96},{1... | collective-permute-start | bytes 442376 | tf_op jit(solution)/shard_map/ppermute | solution.py:298
  76.4 7.4 %copy-start.2 = (s32[2,8]{1,0:T(2,128)S(1)}, s32[2,8]{1,0:T(2,128)}, u32[]{:S(2)}) copy-start(s32[2,8]{1,0:T(2,128)} %sources_ref.1) | copy-start | bytes 196
  76.4 7.4 %copy-start.3 = (f32[2,8]{1,0:T(2,128)S(1)}, f32[2,8]{1,0:T(2,128)}, u32[]{:S(2)}) copy-start(f32[2,8]{1,0:T(2,128)} %weights_ref.1) | copy-start | bytes 196
  76.4 7.4 %copy-start.4 = (s32[2,8]{1,0:T(2,128)S(1)}, s32[2,8]{1,0:T(2,128)}, u32[]{:S(2)}) copy-start(s32[2,8]{1,0:T(2,128)} %flips_ref.1) | copy-start | bytes 196
  76.4 14.3 %collective-permute-start.14 = (bf16[192,384]{1,0:T(8,128)(2,1)S(1)}, bf16[192,384]{1,0:T(8,128)(2,1)S(1)}, u32[]{:S(2)}, u32[]{:S(2)}) collective-permute-start(bf16[192,384]{1,0:T(8,128)(2,1)S(1)} %get-tuple-element.14), channel_id=1, source_target_pairs={{0,16},{16,32},{32,48},{48,0},{64,80},{80,96},{96,112},{112,64},{1... | collective-permute-start | bytes 442376 | tf_op jit(solution)/shard_map/ppermute | solution.py:298
where the time goes:
time: 91.7 us; the launch traced here: 91.6 us
  starting transfers between devices  49.9 us (54%)
  Pallas kernels  31.4 us (34%)
  waiting for transfers between devices  8.36 us (9%)
  local copies, waits for them, and re-layouts  1.28 us (1%)
    ppermute x9, starting transfers between devices, aux(): return lax.ppermute(value, 'aux', aux_shift(dx, dz))  31.3 us
    pallas_call x7, Pallas kernels, ladder(): pl.pallas_call(kernel, out_shape=shapes, in_specs=[VMEM] * ins, out_specs...  26.4 us
    ppermute x6, starting transfers between devices, pair(): return lax.ppermute(value, 'pair', pair_flip(mask))  18.6 us
    ppermute x9, waiting for transfers between devices, aux(): return lax.ppermute(value, 'aux', aux_shift(dx, dz))  5.51 us
    ppermute x6, waiting for transfers between devices, pair(): return lax.ppermute(value, 'pair', pair_flip(mask))  2.85 us
    pallas_call x1, Pallas kernels, couple(): pl.pallas_call(couple_kernel, out_shape=jax.ShapeDtypeStruct((V, W), jnp....  2.01 us
  transfers between devices with their start and end apart: 15, of which 3 were waited for; matrix products, arithmetic and copies ran while one was open for 0% of the time, Pallas kernels for 31%

commit v1 on v0

--- a/solution.py
+++ b/solution.py
@@ -24,8 +24,8 @@
     return pl.CostEstimate(flops=flops, bytes_accessed=bytes_accessed, transcendentals=0)
 
 
-def aux_shift(dx, dz):
-    return [(x * ZH + z, (x + dx) % X * ZH + (z + dz) % ZH) for x in range(X) for z in range(ZH)]
+def aux_flip(mask):
+    return [(a, a ^ mask) for a in range(X * ZH)]
 
 
 def pair_flip(mask):
@@ -294,18 +294,18 @@
 def local(amplitudes, factors, sources, weights, flips):
     where = lax.axis_index("pair").astype(jnp.int32).reshape(1)
 
-    def aux(value, dx, dz):
-        return lax.ppermute(value, "aux", aux_shift(dx, dz))
+    def aux(value, mask):
+        return lax.ppermute(value, "aux", aux_flip(mask))
 
     def pair(value, mask):
         return lax.ppermute(value, "pair", pair_flip(mask))
 
     pack = prep_amp(amplitudes)
-    across, below, above = aux(pack, 0, 2), aux(pack, 0, 1), aux(pack, 0, 3)
+    across, below, above = aux(pack, 2), aux(pack, 1), aux(pack, 3)
     own, other = prep_fac(where % C, factors)
-    left, right = aux(own, 1, 0), aux(own, 3, 0)
+    left, right = aux(own, ZH), aux(own, 3 * ZH)
     self_total = ladder([pack], [own, other], [], False, 4)
-    facing = aux(own, 2, 0)
+    facing = aux(own, 2 * ZH)
     mates = jnp.stack([pack, pair(pack, 2)])
     rest = [across, below, above]
     total = ladder(rest, [own, other], [], False, 4)
@@ -319,7 +319,7 @@
     total = ladder(rest, [facing], [(total, i) for i in range(3)], False, 4)
     far = pair(near, 1)
     back = ladder(rest, [facing_other], [(total, i) for i in range(3)], True, 4)
-    parts = (aux(back[0], 0, 2), aux(back[1], 0, 3), aux(back[2], 0, 1))
+    parts = (aux(back[0], 2), aux(back[1], 1), aux(back[2], 3))
     mine = ladder([pack], [sides_other, facing, facing_other], [(total4, 3)], False, 4)
     coupled = couple(where, sources, weights, flips, near, far)
     return finish(mine, coupled, parts)

time: 91.7 us -> 79.6 us (0.87)
  starting transfers between devices: 49.9 us -> 37.8 us
    ppermute x9, starting transfers between devices: 31.3 us -> 19 us  [aux(): return lax.ppermute(value, 'aux', aux_flip(mask))]
  transfers between devices with their start and end apart: 15 -> 15, of which waited for: 3 -> 4; matrix products, arithmetic and copies ran while one was open for 0% -> 1% of each run, Pallas kernels for 31% -> 36%
where the time goes in v1:
time: 79.6 us; the launch traced here: 79.5 us
  starting transfers between devices  37.8 us (47%)
  Pallas kernels  31.4 us (39%)
  waiting for transfers between devices  8.42 us (11%)
  local copies, waits for them, and re-layouts  1.28 us (2%)
    pallas_call x7, Pallas kernels, ladder(): pl.pallas_call(kernel, out_shape=shapes, in_specs=[VMEM] * ins, out_specs...  26.4 us
    ppermute x9, starting transfers between devices, aux(): return lax.ppermute(value, 'aux', aux_flip(mask))  19 us
    ppermute x6, starting transfers between devices, pair(): return lax.ppermute(value, 'pair', pair_flip(mask))  18.8 us
    ppermute x9, waiting for transfers between devices, aux(): return lax.ppermute(value, 'aux', aux_flip(mask))  6.04 us
    ppermute x6, waiting for transfers between devices, pair(): return lax.ppermute(value, 'pair', pair_flip(mask))  2.38 us
    pallas_call x1, Pallas kernels, couple(): pl.pallas_call(couple_kernel, out_shape=jax.ShapeDtypeStruct((V, W), jnp....  2.01 us
    pallas_call x1, Pallas kernels, prep_fac(): pl.pallas_call(prep_fac_kernel, out_shape=(packs, packs), in_specs=[SMEM,...  1.8 us
  transfers between devices with their start and end apart: 15, of which 4 were waited for; matrix products, arithmetic and copies ran while one was open for 1% of the time, Pallas kernels for 36%

profile of v1, /device:TPU:1, one launch (start us, length us, event | category | flops | bytes accessed | tf_op | source)
XLA Modules:
  0.0 79.5 jit_solution(16049880308620324904)
XLA Ops:
  0.0 1.3 %copy-done = bf16[16,36864]{1,0:T(8,128)(2,1)S(1)} copy-done((bf16[16,36864]{1,0:T(8,128)(2,1)S(1)}, bf16[16,36864]{1,0:T(8,128)(2,1)}, u32[]{:S(2)}) %copy-start) | copy-done | bytes 1179672
  1.3 1.8 %prep_fac.1 = (bf16[4,192,384]{2,1,0:T(8,128)(2,1)S(1)}, bf16[4,192,384]{2,1,0:T(8,128)(2,1)S(1)}) custom-call(s32[1]{0:T(128)S(6)} %select_n.7.core_ref, bf16[16,36864]{1,0:T(8,128)(2,1)S(1)} %copy-done), custom_call_target="tpu_custom_call" | custom-call | bytes 6291456 | tf_op jit(solution)/shard_map/prep_fac/pallas_call | solution.py:101
  3.1 3.4 %collective-permute-start.1 = (bf16[4,192,384]{2,1,0:T(8,128)(2,1)S(1)}, bf16[4,192,384]{2,1,0:T(8,128)(2,1)S(1)}, u32[]{:S(2)}, u32[]{:S(2)}) collective-permute-start(bf16[4,192,384]{2,1,0:T(8,128)(2,1)S(1)} %get-tuple-element.10.refs_3_.refs_1_), channel_id=1, source_target_pairs={{0,192},{16,208},{32,224},{48,240},{64,128},{80,144},{96,160},{112... | collective-permute-start | bytes 1769480 | tf_op jit(solution)/shard_map/ppermute | solution.py:298
  6.5 0.2 prep_amp.1.refs_0_.refs_3_
  6.7 1.7 %collective-permute-start.8 = (bf16[192,384]{1,0:T(8,128)(2,1)S(1)}, bf16[192,384]{1,0:T(8,128)(2,1)S(1)}, u32[]{:S(2)}, u32[]{:S(2)}) collective-permute-start(bf16[192,384]{1,0:T(8,128)(2,1)S(1)} %prep_amp.1.refs_0_.refs_3_), channel_id=1, source_target_pairs={{0,2},{1,3},{2,0},{3,1},{4,6},{5,7},{6,4},{7,5},{8,10},{9,11},{10,... | collective-permute-start | bytes 442376 | tf_op jit(solution)/shard_map/ppermute | solution.py:301
  8.4 5.1 %collective-permute-start.7 = (bf16[192,384]{1,0:T(8,128)(2,1)S(1)}, bf16[192,384]{1,0:T(8,128)(2,1)S(1)}, u32[]{:S(2)}, u32[]{:S(2)}) collective-permute-start(bf16[192,384]{1,0:T(8,128)(2,1)S(1)} %prep_amp.1.refs_0_.refs_3_), channel_id=1, source_target_pairs={{0,48},{16,32},{32,16},{48,0},{64,112},{80,96},{96,80},{112,64},{1... | collective-permute-start | bytes 442376 | tf_op jit(solution)/shard_map/ppermute | solution.py:298
  13.6 1.2 %collective-permute-start.6 = (bf16[192,384]{1,0:T(8,128)(2,1)S(1)}, bf16[192,384]{1,0:T(8,128)(2,1)S(1)}, u32[]{:S(2)}, u32[]{:S(2)}) collective-permute-start(bf16[192,384]{1,0:T(8,128)(2,1)S(1)} %prep_amp.1.refs_0_.refs_3_), channel_id=1, source_target_pairs={{0,16},{16,0},{32,48},{48,32},{64,80},{80,64},{96,112},{112,96},{1... | collective-permute-start | bytes 442376 | tf_op jit(solution)/shard_map/ppermute | solution.py:298
  14.7 2.1 %shard_map.56.refs_7_ = f32[1,192,384]{2,1,0:T(8,128)S(1)} custom-call(bf16[192,384]{1,0:T(8,128)(2,1)S(1)} %prep_amp.1.refs_0_.refs_3_, bf16[4,192,384]{2,1,0:T(8,128)(2,1)S(1)} %get-tuple-element.10.refs_3_.refs_1_, bf16[4,192,384]{2,1,0:T(8,128)(2,1)S(1)} %get-tuple-element.11.refs_4_.refs_2_), custom_call_target="tpu_custom_call" | custom-call | flops 1811939328 | bytes 1048576 | tf_op jit(solution)/shard_map/pallas_call | solution.py:186
  16.9 1.1 %collective-permute-start.5 = (bf16[192,384]{1,0:T(8,128)(2,1)S(1)}, bf16[192,384]{1,0:T(8,128)(2,1)S(1)}, u32[]{:S(2)}, u32[]{:S(2)}) collective-permute-start(bf16[192,384]{1,0:T(8,128)(2,1)S(1)} %prep_amp.1.refs_0_.refs_3_), channel_id=1, source_target_pairs={{0,32},{16,48},{32,0},{48,16},{64,96},{80,112},{96,64},{112,80},{1... | collective-permute-start | bytes 442376 | tf_op jit(solution)/shard_map/ppermute | solution.py:298
  18.0 0.4 collective-permute-done.1.refs_5_
  18.4 2.5 %collective-permute-start.3 = (bf16[4,192,384]{2,1,0:T(8,128)(2,1)S(1)}, bf16[4,192,384]{2,1,0:T(8,128)(2,1)S(1)}, u32[]{:S(2)}, u32[]{:S(2)}) collective-permute-start(bf16[4,192,384]{2,1,0:T(8,128)(2,1)S(1)} %get-tuple-element.10.refs_3_.refs_1_), channel_id=1, source_target_pairs={{0,128},{16,144},{32,160},{48,176},{64,192},{80,208},{96,224},{112... | collective-permute-start | bytes 1769480 | tf_op jit(solution)/shard_map/ppermute | solution.py:298
  20.9 1.3 %collective-permute-start.9 = (bf16[2,192,384]{2,1,0:T(8,128)(2,1)S(1)}, bf16[2,192,384]{2,1,0:T(8,128)(2,1)S(1)}, u32[]{:S(2)}, u32[]{:S(2)}) collective-permute-start(bf16[2,192,384]{2,1,0:T(8,128)(2,1)S(1)} %pad_maximum_fusion.3), channel_id=1, source_target_pairs={{0,4},{1,5},{2,6},{3,7},{4,0},{5,1},{6,2},{7,3},{8,12},{9,13},{10,... | collective-permute-start | bytes 884744 | tf_op jit(solution)/shard_map/ppermute | solution.py:301
  22.2 0.1 pad_maximum_fusion
  22.3 6.4 %collective-permute-start.2 = (bf16[8,192,384]{2,1,0:T(8,128)(2,1)S(1)}, bf16[8,192,384]{2,1,0:T(8,128)(2,1)S(1)}, u32[]{:S(2)}, u32[]{:S(2)}) collective-permute-start(bf16[8,192,384]{2,1,0:T(8,128)(2,1)S(1)} %pad_maximum_fusion), channel_id=1, source_target_pairs={{0,1},{1,0},{2,3},{3,2},{4,5},{5,4},{6,7},{7,6},{8,9},{9,8},{10,11... | collective-permute-start | bytes 3538952 | tf_op jit(solution)/shard_map/ppermute | solution.py:301
  28.8 0.7 collective-permute-done.5.refs_0_
  29.5 4.6 %shard_map.55.refs_6_ = f32[3,192,384]{2,1,0:T(8,128)S(1)} custom-call(bf16[192,384]{1,0:T(8,128)(2,1)S(1)} %collective-permute-done.5.refs_0_, bf16[192,384]{1,0:T(8,128)(2,1)S(1)} %collective-permute-done.6.refs_1_, bf16[192,384]{1,0:T(8,128)(2,1)S(1)} %collective-permute-done.7.refs_2_, bf16[4,192,384]{2,1,0:T(8,128)(2,1)S(1)} %get-tuple-element.10.refs_3_.refs_1_, ...), custom_call_target="tpu_custom_call" | custom-call | flops 5435817984 | bytes 1048576 | tf_op jit(solution)/shard_map/pallas_call | solution.py:186
  34.1 3.0 %collective-permute-start.10 = (bf16[4,192,384]{2,1,0:T(8,128)(2,1)S(1)}, bf16[4,192,384]{2,1,0:T(8,128)(2,1)S(1)}, u32[]{:S(2)}, u32[]{:S(2)}) collective-permute-start(bf16[4,192,384]{2,1,0:T(8,128)(2,1)S(1)} %pad_maximum_fusion.2), channel_id=1, source_target_pairs={{0,8},{1,9},{2,10},{3,11},{4,12},{5,13},{6,14},{7,15},{8,0},{9,1},... | collective-permute-start | bytes 1769480 | tf_op jit(solution)/shard_map/ppermute | solution.py:301
  37.1 2.7 %collective-permute-start.4 = (bf16[4,192,384]{2,1,0:T(8,128)(2,1)S(1)}, bf16[4,192,384]{2,1,0:T(8,128)(2,1)S(1)}, u32[]{:S(2)}, u32[]{:S(2)}) collective-permute-start(bf16[4,192,384]{2,1,0:T(8,128)(2,1)S(1)} %collective-permute-done.3.refs_2_.refs_3_), channel_id=1, source_target_pairs={{0,1},{1,0},{2,3},{3,2},{4,5},{5,4},{6,7},{7,6},{8,9},{9,8},{10,11... | collective-permute-start | bytes 1769480 | tf_op jit(solution)/shard_map/ppermute | solution.py:301
  39.9 5.9 %shard_map.57.refs_4_ = f32[4,192,384]{2,1,0:T(8,128)S(1)} custom-call(bf16[192,384]{1,0:T(8,128)(2,1)S(1)} %collective-permute-done.5.refs_0_, bf16[192,384]{1,0:T(8,128)(2,1)S(1)} %collective-permute-done.6.refs_1_, bf16[192,384]{1,0:T(8,128)(2,1)S(1)} %collective-permute-done.7.refs_2_, bf16[192,384]{1,0:T(8,128)(2,1)S(1)} %prep_amp.1.refs_0_.refs_3_, ...), custom_call_target="tpu_custom_call" | custom-call | flops 7247757312 | bytes 1048576 | tf_op jit(solution)/shard_map/pallas_call | solution.py:186
  45.8 2.4 %collective-permute-done.10 = bf16[4,192,384]{2,1,0:T(8,128)(2,1)S(1)} collective-permute-done((bf16[4,192,384]{2,1,0:T(8,128)(2,1)S(1)}, bf16[4,192,384]{2,1,0:T(8,128)(2,1)S(1)}, u32[]{:S(2)}, u32[]{:S(2)}) %collective-permute-start.10) | collective-permute-done | bytes 589856 | tf_op jit(solution)/shard_map/ppermute | solution.py:301
  48.2 0.2 pad_maximum_fusion.1.near_ref
  48.3 3.6 %collective-permute-start.11 = (bf16[8,192,384]{2,1,0:T(8,128)(2,1)S(1)}, bf16[8,192,384]{2,1,0:T(8,128)(2,1)S(1)}, u32[]{:S(2)}, u32[]{:S(2)}) collective-permute-start(bf16[8,192,384]{2,1,0:T(8,128)(2,1)S(1)} %pad_maximum_fusion.1.near_ref), channel_id=1, source_target_pairs={{0,1},{1,0},{2,3},{3,2},{4,5},{5,4},{6,7},{7,6},{8,9},{9,8},{10,11... | collective-permute-start | bytes 3538952 | tf_op jit(solution)/shard_map/ppermute | solution.py:301
  51.9 4.4 %shard_map.59.refs_4_ = f32[3,192,384]{2,1,0:T(8,128)S(1)} custom-call(bf16[192,384]{1,0:T(8,128)(2,1)S(1)} %collective-permute-done.5.refs_0_, bf16[192,384]{1,0:T(8,128)(2,1)S(1)} %collective-permute-done.6.refs_1_, bf16[192,384]{1,0:T(8,128)(2,1)S(1)} %collective-permute-done.7.refs_2_, bf16[8,192,384]{2,1,0:T(8,128)(2,1)S(1)} %collective-permute-done.2.refs_1_.refs_3_, ...), custom_call_target="tpu_custom_call" | custom-call | flops 5435817984 | bytes 1048576 | tf_op jit(solution)/shard_map/pallas_call | solution.py:186
  56.4 2.2 %shard_map.60.refs_4_ = f32[3,192,384]{2,1,0:T(8,128)S(1)} custom-call(bf16[192,384]{1,0:T(8,128)(2,1)S(1)} %collective-permute-done.5.refs_0_, bf16[192,384]{1,0:T(8,128)(2,1)S(1)} %collective-permute-done.6.refs_1_, bf16[192,384]{1,0:T(8,128)(2,1)S(1)} %collective-permute-done.7.refs_2_, bf16[4,192,384]{2,1,0:T(8,128)(2,1)S(1)} %collective-permute-done.3.refs_2_.refs_3_, ...), custom_call_target="tpu_custom_call" | custom-call | flops 2717908992 | bytes 1048576 | tf_op jit(solution)/shard_map/pallas_call | solution.py:186
  58.6 2.2 %shard_map.61 = (bf16[192,384]{1,0:T(8,128)(2,1)S(1)}, bf16[192,384]{1,0:T(8,128)(2,1)S(1)}, bf16[192,384]{1,0:T(8,128)(2,1)S(1)}) custom-call(bf16[192,384]{1,0:T(8,128)(2,1)S(1)} %collective-permute-done.5.refs_0_, bf16[192,384]{1,0:T(8,128)(2,1)S(1)} %collective-permute-done.6.refs_1_, bf16[192,384]{1,0:T(8,128)(2,1)S(1)} %collective-permute-done.7.refs_2_, ...), custom_call_target="tpu_custom_call" | custom-call | flops 2717908992 | bytes 1048576 | tf_op jit(solution)/shard_map/pallas_call | solution.py:186
  60.8 2.3 %collective-permute-start.12 = (bf16[192,384]{1,0:T(8,128)(2,1)S(1)}, bf16[192,384]{1,0:T(8,128)(2,1)S(1)}, u32[]{:S(2)}, u32[]{:S(2)}) collective-permute-start(bf16[192,384]{1,0:T(8,128)(2,1)S(1)} %get-tuple-element.12), channel_id=1, source_target_pairs={{0,32},{16,48},{32,0},{48,16},{64,96},{80,112},{96,64},{112,80},{1... | collective-permute-start | bytes 442376 | tf_op jit(solution)/shard_map/ppermute | solution.py:298
  63.1 1.2 %collective-permute-start.13 = (bf16[192,384]{1,0:T(8,128)(2,1)S(1)}, bf16[192,384]{1,0:T(8,128)(2,1)S(1)}, u32[]{:S(2)}, u32[]{:S(2)}) collective-permute-start(bf16[192,384]{1,0:T(8,128)(2,1)S(1)} %get-tuple-element.13), channel_id=1, source_target_pairs={{0,16},{16,0},{32,48},{48,32},{64,80},{80,64},{96,112},{112,96},{1... | collective-permute-start | bytes 442376 | tf_op jit(solution)/shard_map/ppermute | solution.py:298
  64.3 2.3 %collective-permute-start.14 = (bf16[192,384]{1,0:T(8,128)(2,1)S(1)}, bf16[192,384]{1,0:T(8,128)(2,1)S(1)}, u32[]{:S(2)}, u32[]{:S(2)}) collective-permute-start(bf16[192,384]{1,0:T(8,128)(2,1)S(1)} %get-tuple-element.14), channel_id=1, source_target_pairs={{0,48},{16,32},{32,16},{48,0},{64,112},{80,96},{96,80},{112,64},{1... | collective-permute-start | bytes 442376 | tf_op jit(solution)/shard_map/ppermute | solution.py:298
  66.5 5.0 %shard_map.58.own_ref = f32[1,192,384]{2,1,0:T(8,128)S(1)} custom-call(bf16[192,384]{1,0:T(8,128)(2,1)S(1)} %prep_amp.1.refs_0_.refs_3_, bf16[8,192,384]{2,1,0:T(8,128)(2,1)S(1)} %collective-permute-done.2.refs_1_.refs_3_, bf16[4,192,384]{2,1,0:T(8,128)(2,1)S(1)} %collective-permute-done.3.refs_2_.refs_3_, ...), custom_call_target="tpu_custom_call" | custom-call | flops 3623878656 | bytes 1048576 | tf_op jit(solution)/shard_map/pallas_call | solution.py:186
  71.6 2.0 %couple.1.couple_ref = f32[192,384]{1,0:T(8,128)S(1)} custom-call(s32[1]{0:T(128)} %bitcast.where_ref, s32[2,8]{1,0:T(2,128)S(1)} %copy-done.2, f32[2,8]{1,0:T(2,128)S(1)} %copy-done.3, s32[2,8]{1,0:T(2,128)S(1)} %copy-done.4, bf16[8,192,384]{2,1,0:T(8,128)(2,1)S(1)} %pad_maximum_fusion.1.near_ref, bf16[8,192,384]{2,1,0:T(8,128)(2,1)S(1)} %collective-permute-done.11.far_ref), custom_call_target="tpu_custom_call" | custom-call | flops 1048576 | bytes 4194304 | tf_op jit(solution)/shard_map/couple/pallas_call | solution.py:243
  73.6 5.0 %collective-permute-done.13.b_ref = bf16[192,384]{1,0:T(8,128)(2,1)S(1)} collective-permute-done((bf16[192,384]{1,0:T(8,128)(2,1)S(1)}, bf16[192,384]{1,0:T(8,128)(2,1)S(1)}, u32[]{:S(2)}, u32[]{:S(2)}) %collective-permute-start.13) | collective-permute-done | bytes 147488 | tf_op jit(solution)/shard_map/ppermute | solution.py:298
  78.6 1.0 %finish.1 = f32[2,36864]{1,0:T(2,128)} custom-call(f32[1,192,384]{2,1,0:T(8,128)S(1)} %shard_map.58.own_ref, f32[192,384]{1,0:T(8,128)S(1)} %couple.1.couple_ref, bf16[192,384]{1,0:T(8,128)(2,1)S(1)} %collective-permute-done.12.a_ref, bf16[192,384]{1,0:T(8,128)(2,1)S(1)} %collective-permute-done.13.b_ref, bf16[192,384]{1,0:T(8,128)(2,1)S(1)} %collective-permute-done.14.c_ref), custom_call_target="tpu_custom_call" | custom-call | flops 1048576 | bytes 2097152 | tf_op jit(solution)/shard_map/finish/pallas_call | solution.py:279
  (23 shorter events, 0.2 us)
Async XLA Ops:
  0.0 1.3 %copy-start = (bf16[16,36864]{1,0:T(8,128)(2,1)S(1)}, bf16[16,36864]{1,0:T(8,128)(2,1)}, u32[]{:S(2)}) copy-start(bf16[16,36864]{1,0:T(8,128)(2,1)} %fac_ref.1) | copy-start | bytes 3538948
  1.3 5.2 %copy-start.1 = (bf16[2,36864]{1,0:T(2,128)(2,1)S(1)}, bf16[2,36864]{1,0:T(2,128)(2,1)}, u32[]{:S(2)}) copy-start(bf16[2,36864]{1,0:T(2,128)(2,1)} %amp_ref.1) | copy-start | bytes 442372
  3.1 15.4 %collective-permute-start.1 = (bf16[4,192,384]{2,1,0:T(8,128)(2,1)S(1)}, bf16[4,192,384]{2,1,0:T(8,128)(2,1)S(1)}, u32[]{:S(2)}, u32[]{:S(2)}) collective-permute-start(bf16[4,192,384]{2,1,0:T(8,128)(2,1)S(1)} %get-tuple-element.10.refs_3_.refs_1_), channel_id=1, source_target_pairs={{0,192},{16,208},{32,224},{48,240},{64,128},{80,144},{96,160},{112... | collective-permute-start | bytes 1769480 | tf_op jit(solution)/shard_map/ppermute | solution.py:298
  6.5 14.4 %collective-permute-start = (bf16[4,192,384]{2,1,0:T(8,128)(2,1)S(1)}, bf16[4,192,384]{2,1,0:T(8,128)(2,1)S(1)}, u32[]{:S(2)}, u32[]{:S(2)}) collective-permute-start(bf16[4,192,384]{2,1,0:T(8,128)(2,1)S(1)} %get-tuple-element.10.refs_3_.refs_1_), channel_id=1, source_target_pairs={{0,64},{16,80},{32,96},{48,112},{64,0},{80,16},{96,32},{112,48},{1... | collective-permute-start | bytes 1769480 | tf_op jit(solution)/shard_map/ppermute | solution.py:298
  6.7 10.2 %collective-permute-start.8 = (bf16[192,384]{1,0:T(8,128)(2,1)S(1)}, bf16[192,384]{1,0:T(8,128)(2,1)S(1)}, u32[]{:S(2)}, u32[]{:S(2)}) collective-permute-start(bf16[192,384]{1,0:T(8,128)(2,1)S(1)} %prep_amp.1.refs_0_.refs_3_), channel_id=1, source_target_pairs={{0,2},{1,3},{2,0},{3,1},{4,6},{5,7},{6,4},{7,5},{8,10},{9,11},{10,... | collective-permute-start | bytes 442376 | tf_op jit(solution)/shard_map/ppermute | solution.py:301
  8.4 13.9 %collective-permute-start.7 = (bf16[192,384]{1,0:T(8,128)(2,1)S(1)}, bf16[192,384]{1,0:T(8,128)(2,1)S(1)}, u32[]{:S(2)}, u32[]{:S(2)}) collective-permute-start(bf16[192,384]{1,0:T(8,128)(2,1)S(1)} %prep_amp.1.refs_0_.refs_3_), channel_id=1, source_target_pairs={{0,48},{16,32},{32,16},{48,0},{64,112},{80,96},{96,80},{112,64},{1... | collective-permute-start | bytes 442376 | tf_op jit(solution)/shard_map/ppermute | solution.py:298
  13.6 15.2 %collective-permute-start.6 = (bf16[192,384]{1,0:T(8,128)(2,1)S(1)}, bf16[192,384]{1,0:T(8,128)(2,1)S(1)}, u32[]{:S(2)}, u32[]{:S(2)}) collective-permute-start(bf16[192,384]{1,0:T(8,128)(2,1)S(1)} %prep_amp.1.refs_0_.refs_3_), channel_id=1, source_target_pairs={{0,16},{16,0},{32,48},{48,32},{64,80},{80,64},{96,112},{112,96},{1... | collective-permute-start | bytes 442376 | tf_op jit(solution)/shard_map/ppermute | solution.py:298
  16.9 12.6 %collective-permute-start.5 = (bf16[192,384]{1,0:T(8,128)(2,1)S(1)}, bf16[192,384]{1,0:T(8,128)(2,1)S(1)}, u32[]{:S(2)}, u32[]{:S(2)}) collective-permute-start(bf16[192,384]{1,0:T(8,128)(2,1)S(1)} %prep_amp.1.refs_0_.refs_3_), channel_id=1, source_target_pairs={{0,32},{16,48},{32,0},{48,16},{64,96},{80,112},{96,64},{112,80},{1... | collective-permute-start | bytes 442376 | tf_op jit(solution)/shard_map/ppermute | solution.py:298
  18.4 18.7 %collective-permute-start.3 = (bf16[4,192,384]{2,1,0:T(8,128)(2,1)S(1)}, bf16[4,192,384]{2,1,0:T(8,128)(2,1)S(1)}, u32[]{:S(2)}, u32[]{:S(2)}) collective-permute-start(bf16[4,192,384]{2,1,0:T(8,128)(2,1)S(1)} %get-tuple-element.10.refs_3_.refs_1_), channel_id=1, source_target_pairs={{0,128},{16,144},{32,160},{48,176},{64,192},{80,208},{96,224},{112... | collective-permute-start | bytes 1769480 | tf_op jit(solution)/shard_map/ppermute | solution.py:298
  20.9 13.1 %collective-permute-start.9 = (bf16[2,192,384]{2,1,0:T(8,128)(2,1)S(1)}, bf16[2,192,384]{2,1,0:T(8,128)(2,1)S(1)}, u32[]{:S(2)}, u32[]{:S(2)}) collective-permute-start(bf16[2,192,384]{2,1,0:T(8,128)(2,1)S(1)} %pad_maximum_fusion.3), channel_id=1, source_target_pairs={{0,4},{1,5},{2,6},{3,7},{4,0},{5,1},{6,2},{7,3},{8,12},{9,13},{10,... | collective-permute-start | bytes 884744 | tf_op jit(solution)/shard_map/ppermute | solution.py:301
  22.3 29.6 %collective-permute-start.2 = (bf16[8,192,384]{2,1,0:T(8,128)(2,1)S(1)}, bf16[8,192,384]{2,1,0:T(8,128)(2,1)S(1)}, u32[]{:S(2)}, u32[]{:S(2)}) collective-permute-start(bf16[8,192,384]{2,1,0:T(8,128)(2,1)S(1)} %pad_maximum_fusion), channel_id=1, source_target_pairs={{0,1},{1,0},{2,3},{3,2},{4,5},{5,4},{6,7},{7,6},{8,9},{9,8},{10,11... | collective-permute-start | bytes 3538952 | tf_op jit(solution)/shard_map/ppermute | solution.py:301
  34.1 14.0 %collective-permute-start.10 = (bf16[4,192,384]{2,1,0:T(8,128)(2,1)S(1)}, bf16[4,192,384]{2,1,0:T(8,128)(2,1)S(1)}, u32[]{:S(2)}, u32[]{:S(2)}) collective-permute-start(bf16[4,192,384]{2,1,0:T(8,128)(2,1)S(1)} %pad_maximum_fusion.2), channel_id=1, source_target_pairs={{0,8},{1,9},{2,10},{3,11},{4,12},{5,13},{6,14},{7,15},{8,0},{9,1},... | collective-permute-start | bytes 1769480 | tf_op jit(solution)/shard_map/ppermute | solution.py:301
  37.1 21.4 %collective-permute-start.4 = (bf16[4,192,384]{2,1,0:T(8,128)(2,1)S(1)}, bf16[4,192,384]{2,1,0:T(8,128)(2,1)S(1)}, u32[]{:S(2)}, u32[]{:S(2)}) collective-permute-start(bf16[4,192,384]{2,1,0:T(8,128)(2,1)S(1)} %collective-permute-done.3.refs_2_.refs_3_), channel_id=1, source_target_pairs={{0,1},{1,0},{2,3},{3,2},{4,5},{5,4},{6,7},{7,6},{8,9},{9,8},{10,11... | collective-permute-start | bytes 1769480 | tf_op jit(solution)/shard_map/ppermute | solution.py:301
  48.3 23.2 %collective-permute-start.11 = (bf16[8,192,384]{2,1,0:T(8,128)(2,1)S(1)}, bf16[8,192,384]{2,1,0:T(8,128)(2,1)S(1)}, u32[]{:S(2)}, u32[]{:S(2)}) collective-permute-start(bf16[8,192,384]{2,1,0:T(8,128)(2,1)S(1)} %pad_maximum_fusion.1.near_ref), channel_id=1, source_target_pairs={{0,1},{1,0},{2,3},{3,2},{4,5},{5,4},{6,7},{7,6},{8,9},{9,8},{10,11... | collective-permute-start | bytes 3538952 | tf_op jit(solution)/shard_map/ppermute | solution.py:301
  60.8 12.8 %collective-permute-start.12 = (bf16[192,384]{1,0:T(8,128)(2,1)S(1)}, bf16[192,384]{1,0:T(8,128)(2,1)S(1)}, u32[]{:S(2)}, u32[]{:S(2)}) collective-permute-start(bf16[192,384]{1,0:T(8,128)(2,1)S(1)} %get-tuple-element.12), channel_id=1, source_target_pairs={{0,32},{16,48},{32,0},{48,16},{64,96},{80,112},{96,64},{112,80},{1... | collective-permute-start | bytes 442376 | tf_op jit(solution)/shard_map/ppermute | solution.py:298
  63.1 15.5 %collective-permute-start.13 = (bf16[192,384]{1,0:T(8,128)(2,1)S(1)}, bf16[192,384]{1,0:T(8,128)(2,1)S(1)}, u32[]{:S(2)}, u32[]{:S(2)}) collective-permute-start(bf16[192,384]{1,0:T(8,128)(2,1)S(1)} %get-tuple-element.13), channel_id=1, source_target_pairs={{0,16},{16,0},{32,48},{48,32},{64,80},{80,64},{96,112},{112,96},{1... | collective-permute-start | bytes 442376 | tf_op jit(solution)/shard_map/ppermute | solution.py:298
  64.3 7.3 %copy-start.2 = (s32[2,8]{1,0:T(2,128)S(1)}, s32[2,8]{1,0:T(2,128)}, u32[]{:S(2)}) copy-start(s32[2,8]{1,0:T(2,128)} %sources_ref.1) | copy-start | bytes 196
  64.3 7.3 %copy-start.3 = (f32[2,8]{1,0:T(2,128)S(1)}, f32[2,8]{1,0:T(2,128)}, u32[]{:S(2)}) copy-start(f32[2,8]{1,0:T(2,128)} %weights_ref.1) | copy-start | bytes 196
  64.3 7.3 %copy-start.4 = (s32[2,8]{1,0:T(2,128)S(1)}, s32[2,8]{1,0:T(2,128)}, u32[]{:S(2)}) copy-start(s32[2,8]{1,0:T(2,128)} %flips_ref.1) | copy-start | bytes 196
  64.3 14.3 %collective-permute-start.14 = (bf16[192,384]{1,0:T(8,128)(2,1)S(1)}, bf16[192,384]{1,0:T(8,128)(2,1)S(1)}, u32[]{:S(2)}, u32[]{:S(2)}) collective-permute-start(bf16[192,384]{1,0:T(8,128)(2,1)S(1)} %get-tuple-element.14), channel_id=1, source_target_pairs={{0,48},{16,32},{32,16},{48,0},{64,112},{80,96},{96,80},{112,64},{1... | collective-permute-start | bytes 442376 | tf_op jit(solution)/shard_map/ppermute | solution.py:298

commit v2 on v1

--- a/solution.py
+++ b/solution.py
@@ -305,22 +305,23 @@
     own, other = prep_fac(where % C, factors)
     left, right = aux(own, ZH), aux(own, 3 * ZH)
     self_total = ladder([pack], [own, other], [], False, 4)
-    facing = aux(own, 2 * ZH)
+    held, left, right = lax.optimization_barrier((own, left, right))
+    facing = aux(held, 2 * ZH)
     mates = jnp.stack([pack, pair(pack, 2)])
     rest = [across, below, above]
     total = ladder(rest, [own, other], [], False, 4)
     mates = jnp.concatenate([mates, pair(mates, 4)])
     sides_other = pair(jnp.concatenate([left, right]), 1)
-    carried = [(total, 0), (total, 1), (total, 2), (self_total, 0)]
-    total4 = ladder(rest + [pack], [left, right], carried, False, 2)
+    total = ladder(rest, [left, right], [(total, i) for i in range(3)], False, 4)
     near = jnp.concatenate([mates, pair(mates, 8)])
-    total = ladder(rest, [sides_other], [(total4, i) for i in range(3)], False, 4)
+    total = ladder(rest, [sides_other], [(total, i) for i in range(3)], False, 4)
     facing_other = pair(facing, 1)
     total = ladder(rest, [facing], [(total, i) for i in range(3)], False, 4)
     far = pair(near, 1)
     back = ladder(rest, [facing_other], [(total, i) for i in range(3)], True, 4)
     parts = (aux(back[0], 2), aux(back[1], 1), aux(back[2], 3))
-    mine = ladder([pack], [sides_other, facing, facing_other], [(total4, 3)], False, 4)
+    facs = [left, right, sides_other, facing, facing_other]
+    mine = ladder([pack], facs, [(self_total, 0)], False, 4)
     coupled = couple(where, sources, weights, flips, near, far)
     return finish(mine, coupled, parts)
 

time: 79.6 us -> 82.4 us (1.035)
  the two profiles are of different devices: /device:TPU:1 before, /device:TPU:6 now
where the time goes in v2:
time: 82.4 us; the launch traced here: 82 us
  starting transfers between devices  32.4 us (39%)
  Pallas kernels  32.1 us (39%)
  waiting for transfers between devices  15.7 us (19%)
  local copies, waits for them, and re-layouts  1.28 us (2%)
    pallas_call x7, Pallas kernels, ladder(): pl.pallas_call(kernel, out_shape=shapes, in_specs=[VMEM] * ins, out_specs...  27.1 us
    ppermute x9, starting transfers between devices, aux(): return lax.ppermute(value, 'aux', aux_flip(mask))  25.9 us
    ppermute x9, waiting for transfers between devices, aux(): return lax.ppermute(value, 'aux', aux_flip(mask))  13.6 us
    ppermute x6, starting transfers between devices, pair(): return lax.ppermute(value, 'pair', pair_flip(mask))  6.49 us
    ppermute x6, waiting for transfers between devices, pair(): return lax.ppermute(value, 'pair', pair_flip(mask))  2.05 us
    pallas_call x1, Pallas kernels, couple(): pl.pallas_call(couple_kernel, out_shape=jax.ShapeDtypeStruct((V, W), jnp....  2 us
    pallas_call x1, Pallas kernels, prep_fac(): pl.pallas_call(prep_fac_kernel, out_shape=(packs, packs), in_specs=[SMEM,...  1.84 us
  transfers between devices with their start and end apart: 15, of which 5 were waited for; matrix products, arithmetic and copies ran while one was open for 0% of the time, Pallas kernels for 36%

profile of v2, /device:TPU:6, one launch (start us, length us, event | category | flops | bytes accessed | tf_op | source)
XLA Modules:
  0.0 82.0 jit_solution(43616831959388350)
XLA Ops:
  0.0 1.3 %copy-done = bf16[16,36864]{1,0:T(8,128)(2,1)S(1)} copy-done((bf16[16,36864]{1,0:T(8,128)(2,1)S(1)}, bf16[16,36864]{1,0:T(8,128)(2,1)}, u32[]{:S(2)}) %copy-start) | copy-done | bytes 1179672
  1.3 1.8 %prep_fac.1 = (bf16[4,192,384]{2,1,0:T(8,128)(2,1)S(1)}, bf16[4,192,384]{2,1,0:T(8,128)(2,1)S(1)}) custom-call(s32[1]{0:T(128)S(6)} %select_n.7.core_ref, bf16[16,36864]{1,0:T(8,128)(2,1)S(1)} %copy-done), custom_call_target="tpu_custom_call" | custom-call | bytes 6291456 | tf_op jit(solution)/shard_map/prep_fac/pallas_call | solution.py:101
  3.1 2.3 %collective-permute-start.1 = (bf16[4,192,384]{2,1,0:T(8,128)(2,1)S(1)}, bf16[4,192,384]{2,1,0:T(8,128)(2,1)S(1)}, u32[]{:S(2)}, u32[]{:S(2)}) collective-permute-start(bf16[4,192,384]{2,1,0:T(8,128)(2,1)S(1)} %get-tuple-element.16.refs_1_.refs_3_), channel_id=1, source_target_pairs={{0,192},{16,208},{32,224},{48,240},{64,128},{80,144},{96,160},{112... | collective-permute-start | bytes 1769480 | tf_op jit(solution)/shard_map/ppermute | solution.py:298
  5.4 0.2 prep_amp.1.refs_0_
  5.6 1.2 %collective-permute-start.5 = (bf16[192,384]{1,0:T(8,128)(2,1)S(1)}, bf16[192,384]{1,0:T(8,128)(2,1)S(1)}, u32[]{:S(2)}, u32[]{:S(2)}) collective-permute-start(bf16[192,384]{1,0:T(8,128)(2,1)S(1)} %prep_amp.1.refs_0_), channel_id=1, source_target_pairs={{0,2},{1,3},{2,0},{3,1},{4,6},{5,7},{6,4},{7,5},{8,10},{9,11},{10,... | collective-permute-start | bytes 442376 | tf_op jit(solution)/shard_map/ppermute | solution.py:301
  6.8 5.4 %collective-permute-start.11 = (bf16[192,384]{1,0:T(8,128)(2,1)S(1)}, bf16[192,384]{1,0:T(8,128)(2,1)S(1)}, u32[]{:S(2)}, u32[]{:S(2)}) collective-permute-start(bf16[192,384]{1,0:T(8,128)(2,1)S(1)} %prep_amp.1.refs_0_), channel_id=1, source_target_pairs={{0,48},{16,32},{32,16},{48,0},{64,112},{80,96},{96,80},{112,64},{1... | collective-permute-start | bytes 442376 | tf_op jit(solution)/shard_map/ppermute | solution.py:298
  12.2 1.5 %collective-permute-start.10 = (bf16[192,384]{1,0:T(8,128)(2,1)S(1)}, bf16[192,384]{1,0:T(8,128)(2,1)S(1)}, u32[]{:S(2)}, u32[]{:S(2)}) collective-permute-start(bf16[192,384]{1,0:T(8,128)(2,1)S(1)} %prep_amp.1.refs_0_), channel_id=1, source_target_pairs={{0,16},{16,0},{32,48},{48,32},{64,80},{80,64},{96,112},{112,96},{1... | collective-permute-start | bytes 442376 | tf_op jit(solution)/shard_map/ppermute | solution.py:298
  13.7 1.7 %collective-permute-start.6 = (bf16[2,192,384]{2,1,0:T(8,128)(2,1)S(1)}, bf16[2,192,384]{2,1,0:T(8,128)(2,1)S(1)}, u32[]{:S(2)}, u32[]{:S(2)}) collective-permute-start(bf16[2,192,384]{2,1,0:T(8,128)(2,1)S(1)} %pad_maximum_fusion.3), channel_id=1, source_target_pairs={{0,4},{1,5},{2,6},{3,7},{4,0},{5,1},{6,2},{7,3},{8,12},{9,13},{10,... | collective-permute-start | bytes 884744 | tf_op jit(solution)/shard_map/ppermute | solution.py:301
  15.4 2.1 %shard_map.55.refs_6_ = f32[1,192,384]{2,1,0:T(8,128)S(1)} custom-call(bf16[192,384]{1,0:T(8,128)(2,1)S(1)} %prep_amp.1.refs_0_, bf16[4,192,384]{2,1,0:T(8,128)(2,1)S(1)} %get-tuple-element.16.refs_1_.refs_3_, bf16[4,192,384]{2,1,0:T(8,128)(2,1)S(1)} %get-tuple-element.17.refs_2_.refs_4_), custom_call_target="tpu_custom_call" | custom-call | flops 1811939328 | bytes 1048576 | tf_op jit(solution)/shard_map/pallas_call | solution.py:186
  17.5 1.9 %collective-permute-done.1.refs_2_.refs_4_ = bf16[4,192,384]{2,1,0:T(8,128)(2,1)S(1)} collective-permute-done((bf16[4,192,384]{2,1,0:T(8,128)(2,1)S(1)}, bf16[4,192,384]{2,1,0:T(8,128)(2,1)S(1)}, u32[]{:S(2)}, u32[]{:S(2)}) %collective-permute-start.1) | collective-permute-done | bytes 589856 | tf_op jit(solution)/shard_map/ppermute | solution.py:298
  19.4 7.2 %collective-permute-start.9 = (bf16[192,384]{1,0:T(8,128)(2,1)S(1)}, bf16[192,384]{1,0:T(8,128)(2,1)S(1)}, u32[]{:S(2)}, u32[]{:S(2)}) collective-permute-start(bf16[192,384]{1,0:T(8,128)(2,1)S(1)} %prep_amp.1.refs_0_), channel_id=1, source_target_pairs={{0,32},{16,48},{32,0},{48,16},{64,96},{80,112},{96,64},{112,80},{1... | collective-permute-start | bytes 442376 | tf_op jit(solution)/shard_map/ppermute | solution.py:298
  26.6 0.1 pad_maximum_fusion
  26.8 0.1 collective-permute-start.2
  26.9 0.1 pad_maximum_fusion.2
  27.0 3.5 %collective-permute-start.7 = (bf16[4,192,384]{2,1,0:T(8,128)(2,1)S(1)}, bf16[4,192,384]{2,1,0:T(8,128)(2,1)S(1)}, u32[]{:S(2)}, u32[]{:S(2)}) collective-permute-start(bf16[4,192,384]{2,1,0:T(8,128)(2,1)S(1)} %pad_maximum_fusion.2), channel_id=1, source_target_pairs={{0,8},{1,9},{2,10},{3,11},{4,12},{5,13},{6,14},{7,15},{8,0},{9,1},... | collective-permute-start | bytes 1769480 | tf_op jit(solution)/shard_map/ppermute | solution.py:301
  30.4 1.2 %collective-permute-done.9.refs_0_ = bf16[192,384]{1,0:T(8,128)(2,1)S(1)} collective-permute-done((bf16[192,384]{1,0:T(8,128)(2,1)S(1)}, bf16[192,384]{1,0:T(8,128)(2,1)S(1)}, u32[]{:S(2)}, u32[]{:S(2)}) %collective-permute-start.9) | collective-permute-done | bytes 147488 | tf_op jit(solution)/shard_map/ppermute | solution.py:298
  31.7 4.6 %shard_map.57.refs_5_ = f32[3,192,384]{2,1,0:T(8,128)S(1)} custom-call(bf16[192,384]{1,0:T(8,128)(2,1)S(1)} %collective-permute-done.9.refs_0_, bf16[192,384]{1,0:T(8,128)(2,1)S(1)} %collective-permute-done.10.refs_1_, bf16[192,384]{1,0:T(8,128)(2,1)S(1)} %collective-permute-done.11.refs_2_, bf16[4,192,384]{2,1,0:T(8,128)(2,1)S(1)} %get-tuple-element.16.refs_1_.refs_3_, ...), custom_call_target="tpu_custom_call" | custom-call | flops 5435817984 | bytes 1048576 | tf_op jit(solution)/shard_map/pallas_call | solution.py:186
  36.3 1.6 %collective-permute-start.3 = (bf16[4,192,384]{2,1,0:T(8,128)(2,1)S(1)}, bf16[4,192,384]{2,1,0:T(8,128)(2,1)S(1)}, u32[]{:S(2)}, u32[]{:S(2)}) collective-permute-start(bf16[4,192,384]{2,1,0:T(8,128)(2,1)S(1)} %get-tuple-element.16.refs_1_.refs_3_), channel_id=1, source_target_pairs={{0,128},{16,144},{32,160},{48,176},{64,192},{80,208},{96,224},{112... | collective-permute-start | bytes 1769480 | tf_op jit(solution)/shard_map/ppermute | solution.py:298
  37.9 4.6 %shard_map.58.refs_4_ = f32[3,192,384]{2,1,0:T(8,128)S(1)} custom-call(bf16[192,384]{1,0:T(8,128)(2,1)S(1)} %collective-permute-done.9.refs_0_, bf16[192,384]{1,0:T(8,128)(2,1)S(1)} %collective-permute-done.10.refs_1_, bf16[192,384]{1,0:T(8,128)(2,1)S(1)} %collective-permute-done.11.refs_2_, bf16[4,192,384]{2,1,0:T(8,128)(2,1)S(1)} %collective-permute-done.refs_1_.refs_3_, ...), custom_call_target="tpu_custom_call" | custom-call | flops 5435817984 | bytes 1048576 | tf_op jit(solution)/shard_map/pallas_call | solution.py:186
  42.4 2.0 %collective-permute-done.7 = bf16[4,192,384]{2,1,0:T(8,128)(2,1)S(1)} collective-permute-done((bf16[4,192,384]{2,1,0:T(8,128)(2,1)S(1)}, bf16[4,192,384]{2,1,0:T(8,128)(2,1)S(1)}, u32[]{:S(2)}, u32[]{:S(2)}) %collective-permute-start.7) | collective-permute-done | bytes 589856 | tf_op jit(solution)/shard_map/ppermute | solution.py:301
  44.5 0.2 pad_maximum_fusion.1.near_ref
  44.6 0.1 collective-permute-start.8
  44.7 7.3 %collective-permute-done.3.refs_4_.refs_3_ = bf16[4,192,384]{2,1,0:T(8,128)(2,1)S(1)} collective-permute-done((bf16[4,192,384]{2,1,0:T(8,128)(2,1)S(1)}, bf16[4,192,384]{2,1,0:T(8,128)(2,1)S(1)}, u32[]{:S(2)}, u32[]{:S(2)}) %collective-permute-start.3) | collective-permute-done | bytes 589856 | tf_op jit(solution)/shard_map/ppermute | solution.py:298
  52.0 4.4 %shard_map.59.refs_4_ = f32[3,192,384]{2,1,0:T(8,128)S(1)} custom-call(bf16[192,384]{1,0:T(8,128)(2,1)S(1)} %collective-permute-done.9.refs_0_, bf16[192,384]{1,0:T(8,128)(2,1)S(1)} %collective-permute-done.10.refs_1_, bf16[192,384]{1,0:T(8,128)(2,1)S(1)} %collective-permute-done.11.refs_2_, bf16[8,192,384]{2,1,0:T(8,128)(2,1)S(1)} %collective-permute-done.2.refs_3_, ...), custom_call_target="tpu_custom_call" | custom-call | flops 5435817984 | bytes 1048576 | tf_op jit(solution)/shard_map/pallas_call | solution.py:186
  56.5 2.2 %shard_map.60.refs_4_ = f32[3,192,384]{2,1,0:T(8,128)S(1)} custom-call(bf16[192,384]{1,0:T(8,128)(2,1)S(1)} %collective-permute-done.9.refs_0_, bf16[192,384]{1,0:T(8,128)(2,1)S(1)} %collective-permute-done.10.refs_1_, bf16[192,384]{1,0:T(8,128)(2,1)S(1)} %collective-permute-done.11.refs_2_, bf16[4,192,384]{2,1,0:T(8,128)(2,1)S(1)} %collective-permute-done.3.refs_4_.refs_3_, ...), custom_call_target="tpu_custom_call" | custom-call | flops 2717908992 | bytes 1048576 | tf_op jit(solution)/shard_map/pallas_call | solution.py:186
  58.6 2.2 %shard_map.61 = (bf16[192,384]{1,0:T(8,128)(2,1)S(1)}, bf16[192,384]{1,0:T(8,128)(2,1)S(1)}, bf16[192,384]{1,0:T(8,128)(2,1)S(1)}) custom-call(bf16[192,384]{1,0:T(8,128)(2,1)S(1)} %collective-permute-done.9.refs_0_, bf16[192,384]{1,0:T(8,128)(2,1)S(1)} %collective-permute-done.10.refs_1_, bf16[192,384]{1,0:T(8,128)(2,1)S(1)} %collective-permute-done.11.refs_2_, ...), custom_call_target="tpu_custom_call" | custom-call | flops 2717908992 | bytes 1048576 | tf_op jit(solution)/shard_map/pallas_call | solution.py:186
  60.8 3.0 %collective-permute-start.12 = (bf16[192,384]{1,0:T(8,128)(2,1)S(1)}, bf16[192,384]{1,0:T(8,128)(2,1)S(1)}, u32[]{:S(2)}, u32[]{:S(2)}) collective-permute-start(bf16[192,384]{1,0:T(8,128)(2,1)S(1)} %get-tuple-element.18), channel_id=1, source_target_pairs={{0,32},{16,48},{32,0},{48,16},{64,96},{80,112},{96,64},{112,80},{1... | collective-permute-start | bytes 442376 | tf_op jit(solution)/shard_map/ppermute | solution.py:298
  63.8 4.9 %collective-permute-start.13 = (bf16[192,384]{1,0:T(8,128)(2,1)S(1)}, bf16[192,384]{1,0:T(8,128)(2,1)S(1)}, u32[]{:S(2)}, u32[]{:S(2)}) collective-permute-start(bf16[192,384]{1,0:T(8,128)(2,1)S(1)} %get-tuple-element.19), channel_id=1, source_target_pairs={{0,16},{16,0},{32,48},{48,32},{64,80},{80,64},{96,112},{112,96},{1... | collective-permute-start | bytes 442376 | tf_op jit(solution)/shard_map/ppermute | solution.py:298
  68.8 7.1 %shard_map.56.own_ref = f32[1,192,384]{2,1,0:T(8,128)S(1)} custom-call(bf16[192,384]{1,0:T(8,128)(2,1)S(1)} %prep_amp.1.refs_0_, bf16[4,192,384]{2,1,0:T(8,128)(2,1)S(1)} %collective-permute-done.refs_1_.refs_3_, bf16[4,192,384]{2,1,0:T(8,128)(2,1)S(1)} %collective-permute-done.1.refs_2_.refs_4_, bf16[8,192,384]{2,1,0:T(8,128)(2,1)S(1)} %collective-permute-done.2.refs_3_, ...), custom_call_target="tpu_custom_call" | custom-call | flops 5435817984 | bytes 1048576 | tf_op jit(solution)/shard_map/pallas_call | solution.py:186
  75.9 2.0 %couple.1.couple_ref = f32[192,384]{1,0:T(8,128)S(1)} custom-call(s32[1]{0:T(128)} %bitcast.where_ref, s32[2,8]{1,0:T(2,128)S(1)} %copy-done.2, f32[2,8]{1,0:T(2,128)S(1)} %copy-done.3, s32[2,8]{1,0:T(2,128)S(1)} %copy-done.4, bf16[8,192,384]{2,1,0:T(8,128)(2,1)S(1)} %pad_maximum_fusion.1.near_ref, bf16[8,192,384]{2,1,0:T(8,128)(2,1)S(1)} %collective-permute-done.8.far_ref), custom_call_target="tpu_custom_call" | custom-call | flops 1048576 | bytes 4194304 | tf_op jit(solution)/shard_map/couple/pallas_call | solution.py:243
  77.9 3.1 %collective-permute-done.13.b_ref = bf16[192,384]{1,0:T(8,128)(2,1)S(1)} collective-permute-done((bf16[192,384]{1,0:T(8,128)(2,1)S(1)}, bf16[192,384]{1,0:T(8,128)(2,1)S(1)}, u32[]{:S(2)}, u32[]{:S(2)}) %collective-permute-start.13) | collective-permute-done | bytes 147488 | tf_op jit(solution)/shard_map/ppermute | solution.py:298
  81.1 1.0 %finish.1 = f32[2,36864]{1,0:T(2,128)} custom-call(f32[1,192,384]{2,1,0:T(8,128)S(1)} %shard_map.56.own_ref, f32[192,384]{1,0:T(8,128)S(1)} %couple.1.couple_ref, bf16[192,384]{1,0:T(8,128)(2,1)S(1)} %collective-permute-done.12.a_ref, bf16[192,384]{1,0:T(8,128)(2,1)S(1)} %collective-permute-done.13.b_ref, bf16[192,384]{1,0:T(8,128)(2,1)S(1)} %collective-permute-done.14.c_ref), custom_call_target="tpu_custom_call" | custom-call | flops 1048576 | bytes 2097152 | tf_op jit(solution)/shard_map/finish/pallas_call | solution.py:279
  (23 shorter events, 0.1 us)
Async XLA Ops:
  0.0 1.3 %copy-start = (bf16[16,36864]{1,0:T(8,128)(2,1)S(1)}, bf16[16,36864]{1,0:T(8,128)(2,1)}, u32[]{:S(2)}) copy-start(bf16[16,36864]{1,0:T(8,128)(2,1)} %fac_ref.1) | copy-start | bytes 3538948
  1.3 4.1 %copy-start.1 = (bf16[2,36864]{1,0:T(2,128)(2,1)S(1)}, bf16[2,36864]{1,0:T(2,128)(2,1)}, u32[]{:S(2)}) copy-start(bf16[2,36864]{1,0:T(2,128)(2,1)} %amp_ref.1) | copy-start | bytes 442372
  3.1 16.3 %collective-permute-start.1 = (bf16[4,192,384]{2,1,0:T(8,128)(2,1)S(1)}, bf16[4,192,384]{2,1,0:T(8,128)(2,1)S(1)}, u32[]{:S(2)}, u32[]{:S(2)}) collective-permute-start(bf16[4,192,384]{2,1,0:T(8,128)(2,1)S(1)} %get-tuple-element.16.refs_1_.refs_3_), channel_id=1, source_target_pairs={{0,192},{16,208},{32,224},{48,240},{64,128},{80,144},{96,160},{112... | collective-permute-start | bytes 1769480 | tf_op jit(solution)/shard_map/ppermute | solution.py:298
  5.4 21.2 %collective-permute-start = (bf16[4,192,384]{2,1,0:T(8,128)(2,1)S(1)}, bf16[4,192,384]{2,1,0:T(8,128)(2,1)S(1)}, u32[]{:S(2)}, u32[]{:S(2)}) collective-permute-start(bf16[4,192,384]{2,1,0:T(8,128)(2,1)S(1)} %get-tuple-element.16.refs_1_.refs_3_), channel_id=1, source_target_pairs={{0,64},{16,80},{32,96},{48,112},{64,0},{80,16},{96,32},{112,48},{1... | collective-permute-start | bytes 1769480 | tf_op jit(solution)/shard_map/ppermute | solution.py:298
  5.6 8.0 %collective-permute-start.5 = (bf16[192,384]{1,0:T(8,128)(2,1)S(1)}, bf16[192,384]{1,0:T(8,128)(2,1)S(1)}, u32[]{:S(2)}, u32[]{:S(2)}) collective-permute-start(bf16[192,384]{1,0:T(8,128)(2,1)S(1)} %prep_amp.1.refs_0_), channel_id=1, source_target_pairs={{0,2},{1,3},{2,0},{3,1},{4,6},{5,7},{6,4},{7,5},{8,10},{9,11},{10,... | collective-permute-start | bytes 442376 | tf_op jit(solution)/shard_map/ppermute | solution.py:301
  6.8 23.6 %collective-permute-start.11 = (bf16[192,384]{1,0:T(8,128)(2,1)S(1)}, bf16[192,384]{1,0:T(8,128)(2,1)S(1)}, u32[]{:S(2)}, u32[]{:S(2)}) collective-permute-start(bf16[192,384]{1,0:T(8,128)(2,1)S(1)} %prep_amp.1.refs_0_), channel_id=1, source_target_pairs={{0,48},{16,32},{32,16},{48,0},{64,112},{80,96},{96,80},{112,64},{1... | collective-permute-start | bytes 442376 | tf_op jit(solution)/shard_map/ppermute | solution.py:298
  12.2 18.2 %collective-permute-start.10 = (bf16[192,384]{1,0:T(8,128)(2,1)S(1)}, bf16[192,384]{1,0:T(8,128)(2,1)S(1)}, u32[]{:S(2)}, u32[]{:S(2)}) collective-permute-start(bf16[192,384]{1,0:T(8,128)(2,1)S(1)} %prep_amp.1.refs_0_), channel_id=1, source_target_pairs={{0,16},{16,0},{32,48},{48,32},{64,80},{80,64},{96,112},{112,96},{1... | collective-permute-start | bytes 442376 | tf_op jit(solution)/shard_map/ppermute | solution.py:298
  13.7 13.2 %collective-permute-start.6 = (bf16[2,192,384]{2,1,0:T(8,128)(2,1)S(1)}, bf16[2,192,384]{2,1,0:T(8,128)(2,1)S(1)}, u32[]{:S(2)}, u32[]{:S(2)}) collective-permute-start(bf16[2,192,384]{2,1,0:T(8,128)(2,1)S(1)} %pad_maximum_fusion.3), channel_id=1, source_target_pairs={{0,4},{1,5},{2,6},{3,7},{4,0},{5,1},{6,2},{7,3},{8,12},{9,13},{10,... | collective-permute-start | bytes 884744 | tf_op jit(solution)/shard_map/ppermute | solution.py:301
  19.4 12.2 %collective-permute-start.9 = (bf16[192,384]{1,0:T(8,128)(2,1)S(1)}, bf16[192,384]{1,0:T(8,128)(2,1)S(1)}, u32[]{:S(2)}, u32[]{:S(2)}) collective-permute-start(bf16[192,384]{1,0:T(8,128)(2,1)S(1)} %prep_amp.1.refs_0_), channel_id=1, source_target_pairs={{0,32},{16,48},{32,0},{48,16},{64,96},{80,112},{96,64},{112,80},{1... | collective-permute-start | bytes 442376 | tf_op jit(solution)/shard_map/ppermute | solution.py:298
  26.8 25.3 %collective-permute-start.2 = (bf16[8,192,384]{2,1,0:T(8,128)(2,1)S(1)}, bf16[8,192,384]{2,1,0:T(8,128)(2,1)S(1)}, u32[]{:S(2)}, u32[]{:S(2)}) collective-permute-start(bf16[8,192,384]{2,1,0:T(8,128)(2,1)S(1)} %pad_maximum_fusion), channel_id=1, source_target_pairs={{0,1},{1,0},{2,3},{3,2},{4,5},{5,4},{6,7},{7,6},{8,9},{9,8},{10,11... | collective-permute-start | bytes 3538952 | tf_op jit(solution)/shard_map/ppermute | solution.py:301
  27.0 17.5 %collective-permute-start.7 = (bf16[4,192,384]{2,1,0:T(8,128)(2,1)S(1)}, bf16[4,192,384]{2,1,0:T(8,128)(2,1)S(1)}, u32[]{:S(2)}, u32[]{:S(2)}) collective-permute-start(bf16[4,192,384]{2,1,0:T(8,128)(2,1)S(1)} %pad_maximum_fusion.2), channel_id=1, source_target_pairs={{0,8},{1,9},{2,10},{3,11},{4,12},{5,13},{6,14},{7,15},{8,0},{9,1},... | collective-permute-start | bytes 1769480 | tf_op jit(solution)/shard_map/ppermute | solution.py:301
  36.3 15.8 %collective-permute-start.3 = (bf16[4,192,384]{2,1,0:T(8,128)(2,1)S(1)}, bf16[4,192,384]{2,1,0:T(8,128)(2,1)S(1)}, u32[]{:S(2)}, u32[]{:S(2)}) collective-permute-start(bf16[4,192,384]{2,1,0:T(8,128)(2,1)S(1)} %get-tuple-element.16.refs_1_.refs_3_), channel_id=1, source_target_pairs={{0,128},{16,144},{32,160},{48,176},{64,192},{80,208},{96,224},{112... | collective-permute-start | bytes 1769480 | tf_op jit(solution)/shard_map/ppermute | solution.py:298
  44.6 31.3 %collective-permute-start.8 = (bf16[8,192,384]{2,1,0:T(8,128)(2,1)S(1)}, bf16[8,192,384]{2,1,0:T(8,128)(2,1)S(1)}, u32[]{:S(2)}, u32[]{:S(2)}) collective-permute-start(bf16[8,192,384]{2,1,0:T(8,128)(2,1)S(1)} %pad_maximum_fusion.1.near_ref), channel_id=1, source_target_pairs={{0,1},{1,0},{2,3},{3,2},{4,5},{5,4},{6,7},{7,6},{8,9},{9,8},{10,11... | collective-permute-start | bytes 3538952 | tf_op jit(solution)/shard_map/ppermute | solution.py:301
  52.0 6.6 %collective-permute-start.4 = (bf16[4,192,384]{2,1,0:T(8,128)(2,1)S(1)}, bf16[4,192,384]{2,1,0:T(8,128)(2,1)S(1)}, u32[]{:S(2)}, u32[]{:S(2)}) collective-permute-start(bf16[4,192,384]{2,1,0:T(8,128)(2,1)S(1)} %collective-permute-done.3.refs_4_.refs_3_), channel_id=1, source_target_pairs={{0,1},{1,0},{2,3},{3,2},{4,5},{5,4},{6,7},{7,6},{8,9},{9,8},{10,11... | collective-permute-start | bytes 1769480 | tf_op jit(solution)/shard_map/ppermute | solution.py:301
  60.8 17.1 %collective-permute-start.12 = (bf16[192,384]{1,0:T(8,128)(2,1)S(1)}, bf16[192,384]{1,0:T(8,128)(2,1)S(1)}, u32[]{:S(2)}, u32[]{:S(2)}) collective-permute-start(bf16[192,384]{1,0:T(8,128)(2,1)S(1)} %get-tuple-element.18), channel_id=1, source_target_pairs={{0,32},{16,48},{32,0},{48,16},{64,96},{80,112},{96,64},{112,80},{1... | collective-permute-start | bytes 442376 | tf_op jit(solution)/shard_map/ppermute | solution.py:298
  63.8 17.2 %collective-permute-start.13 = (bf16[192,384]{1,0:T(8,128)(2,1)S(1)}, bf16[192,384]{1,0:T(8,128)(2,1)S(1)}, u32[]{:S(2)}, u32[]{:S(2)}) collective-permute-start(bf16[192,384]{1,0:T(8,128)(2,1)S(1)} %get-tuple-element.19), channel_id=1, source_target_pairs={{0,16},{16,0},{32,48},{48,32},{64,80},{80,64},{96,112},{112,96},{1... | collective-permute-start | bytes 442376 | tf_op jit(solution)/shard_map/ppermute | solution.py:298
  68.8 7.1 %copy-start.2 = (s32[2,8]{1,0:T(2,128)S(1)}, s32[2,8]{1,0:T(2,128)}, u32[]{:S(2)}) copy-start(s32[2,8]{1,0:T(2,128)} %sources_ref.1) | copy-start | bytes 196
  68.8 7.1 %copy-start.3 = (f32[2,8]{1,0:T(2,128)S(1)}, f32[2,8]{1,0:T(2,128)}, u32[]{:S(2)}) copy-start(f32[2,8]{1,0:T(2,128)} %weights_ref.1) | copy-start | bytes 196
  68.8 7.1 %copy-start.4 = (s32[2,8]{1,0:T(2,128)S(1)}, s32[2,8]{1,0:T(2,128)}, u32[]{:S(2)}) copy-start(s32[2,8]{1,0:T(2,128)} %flips_ref.1) | copy-start | bytes 196
  68.8 12.3 %collective-permute-start.14 = (bf16[192,384]{1,0:T(8,128)(2,1)S(1)}, bf16[192,384]{1,0:T(8,128)(2,1)S(1)}, u32[]{:S(2)}, u32[]{:S(2)}) collective-permute-start(bf16[192,384]{1,0:T(8,128)(2,1)S(1)} %get-tuple-element.20), channel_id=1, source_target_pairs={{0,48},{16,32},{32,16},{48,0},{64,112},{80,96},{96,80},{112,64},{1... | collective-permute-start | bytes 442376 | tf_op jit(solution)/shard_map/ppermute | solution.py:298
